TPU v7x, 768 devices: a whole 4x8x12 slice. The times are simulated.
768 devices in a mesh: section: 48 (over y_hi, z), tensor: 16 (over y_lo, x, core).
Axes of the slice: x: 4, y: 8 (y_hi: 4, y_lo: 2; y = y_hi * 2 + y_lo), z: 12, core: 2. Of those that a mesh axis runs over, the one named last changes fastest.
Arguments:
- layer_input: bfloat16 [48, 512, 6144], P('section', None, 'tensor'), may hold values from -200 to 200
- grad_input: bfloat16 [48, 512, 6144], P('section', None, 'tensor'), may hold values from -8 to 8
- stashed: bfloat16 [48, 2, 512, 6144], P('section', None, None, 'tensor'), may hold values from -200 to 200
- eviction: int32 [48], P('section'), may hold values from 0 to 1, as said below
- query_gain: float32 [48, 6144], P('section', 'tensor'), may hold values from 0.5 to 2
- key_gain: float32 [48, 6144], P('section', 'tensor'), may hold values from 0.5 to 2
Outputs:
- layer_output: bfloat16 [48, 512, 6144], P('section', None, 'tensor')
- grad_output: bfloat16 [48, 512, 6144], P('section', None, 'tensor')
Inputs may be any that keep to these rules, and one draw needn't show every extreme that they name: `eviction`: section 0 always evicts.
All inputs are finite; a program needn't handle non-finite values.
Results may differ from a plain program's by a relative error of at most 0.0078.
Values may be sent and summed in bfloat16 or wider, within the bound.
A program may use at most 32 MiB of HBM per device.

v0:
```python
import math

import jax
import jax.numpy as jnp
from jax import lax
from jax.sharding import PartitionSpec as P

HDIM = 128
DW = 6144


EPSILON = 1e-05


def passed_along(x, axis, by):
    size = lax.axis_size(axis)
    return lax.ppermute(x, axis, [(i, (i + by) % size) for i in range(size)])


def local_squares(activations):
    widened = activations.astype(jnp.float32)
    return jnp.sum(widened * widened, axis=-1)


def normalize(activations, square_total, gain_query, gain_key):
    widened = activations.astype(jnp.float32)
    factor = lax.rsqrt(square_total / DW + EPSILON)
    normed = widened * factor[:, None]
    queries = (normed * gain_query).astype(jnp.bfloat16)
    keys_all = (normed * gain_key).astype(jnp.bfloat16)
    values = normed.astype(jnp.bfloat16)
    return (widened, factor, queries, keys_all, values)


def split_heads(matrix):
    return matrix.reshape(matrix.shape[0], matrix.shape[1] // HDIM, HDIM)


def attention_weights(query_heads, key_heads):
    length = query_heads.shape[0]
    scores = jnp.einsum(
        "qhd,khd->hqk", query_heads, key_heads, preferred_element_type=jnp.float32
    ) * (1.0 / math.sqrt(HDIM))
    causal = jnp.arange(length)[:, None] >= jnp.arange(length)[None, :]
    scores = jnp.where(causal[None], scores, -1e30)
    shifted = scores - jnp.max(scores, axis=-1, keepdims=True)
    exponent = jnp.exp(shifted)
    return exponent / jnp.sum(exponent, axis=-1, keepdims=True)


def forward_layer(activations, square_total, gain_query, gain_key):
    widened, factor, queries, keys_all, values = normalize(
        activations, square_total, gain_query, gain_key
    )
    weights = attention_weights(split_heads(queries), split_heads(keys_all))
    rounded = weights.astype(jnp.bfloat16)
    mixed_heads = jnp.einsum(
        "hqk,khd->qhd", rounded, split_heads(values), preferred_element_type=jnp.float32
    )
    return (widened + mixed_heads.reshape(widened.shape)).astype(jnp.bfloat16)


def backward_terms(activations, square_total, upstream, gain_query, gain_key):
    widened, factor, queries, keys_all, values = normalize(
        activations, square_total, gain_query, gain_key
    )
    query_heads = split_heads(queries)
    key_heads = split_heads(keys_all)
    weights = attention_weights(query_heads, key_heads)
    rounded = weights.astype(jnp.bfloat16)
    grad_heads = split_heads(upstream)
    d_values = jnp.einsum("hqk,qhd->khd", rounded, grad_heads, preferred_element_type=jnp.float32)
    d_weights = jnp.einsum(
        "qhd,khd->hqk", grad_heads, split_heads(values), preferred_element_type=jnp.float32
    )
    row_delta = jnp.sum(weights * d_weights, axis=-1, keepdims=True)
    d_scores = (weights * (d_weights - row_delta) * (1.0 / math.sqrt(HDIM))).astype(jnp.bfloat16)
    d_queries = jnp.einsum("hqk,khd->qhd", d_scores, key_heads, preferred_element_type=jnp.float32)
    d_keys = jnp.einsum("hqk,qhd->khd", d_scores, query_heads, preferred_element_type=jnp.float32)
    flat_shape = widened.shape
    d_normed = (
        d_queries.reshape(flat_shape) * gain_query
        + d_keys.reshape(flat_shape) * gain_key
        + d_values.reshape(flat_shape)
    )
    partial_inner = jnp.sum(d_normed * widened, axis=-1)
    return (widened, factor, d_normed, partial_inner)


def local(layer_input, grad_input, stashed, eviction, query_gain, key_gain):
    half_sections = lax.axis_size("section") // 2
    current = layer_input[0]
    upstream = grad_input[0]
    gain_query = query_gain[0]
    gain_key = key_gain[0]
    fetched = passed_along(stashed[0, 1], "section", -half_sections)
    chosen = jnp.where(eviction[0] == 1, fetched, stashed[0, 0])
    forward_total = lax.psum(local_squares(current), "tensor")
    recompute_total = lax.psum(local_squares(chosen), "tensor")
    output = forward_layer(current, forward_total, gain_query, gain_key)
    widened, factor, d_normed, partial_inner = backward_terms(
        chosen, recompute_total, upstream, gain_query, gain_key
    )
    inner_sum = lax.psum(partial_inner, "tensor")
    result = (
        upstream.astype(jnp.float32)
        + factor[:, None] * d_normed
        - widened * (factor**3)[:, None] * inner_sum[:, None] / DW
    )
    result = result.astype(jnp.bfloat16)
    passed = passed_along(result, "section", -1)
    return (output[None], passed[None])


def solution(mesh):
    placed = (
        P("section", None, "tensor"),
        P("section", None, "tensor"),
        P("section", None, None, "tensor"),
        P("section"),
        P("section", "tensor"),
        P("section", "tensor"),
    )
    return jax.shard_map(
        local,
        mesh=mesh,
        in_specs=placed,
        out_specs=(P("section", None, "tensor"), P("section", None, "tensor")),
        check_vma=False,
    )
```

profile of v0, /device:TPU:8, one launch (start us, length us, event | category | flops | bytes accessed | tf_op | source)
XLA Modules:
  0.0 138.2 jit_solution(15667109095011829331)
XLA Ops:
  0.6 0.0 copy-start.4
  0.6 0.0 copy-start.5
  0.7 0.0 copy-start
  0.7 0.0 copy-start.1
  0.7 1.3 fusion.48
  1.9 0.2 copy.53
  2.1 6.8 %collective-permute-start = (bf16[512,384]{0,1:T(8,128)(2,1)S(1)}, bf16[512,384]{0,1:T(8,128)(2,1)S(1)}, u32[]{:S(2)}, u32[]{:S(2)}) collective-permute-start(bf16[512,384]{0,1:T(8,128)(2,1)S(1)} %bitcast.79), channel_id=1, source_target_pairs={{0,384},{16,400},{32,416},{48,432},{64,448},{80,464},{96,480},{112... | collective-permute-start | bytes 1179656 | tf_op jit(solution)/shard_map/ppermute | solution.py:17
  9.0 0.2 copy.54
  9.8 0.0 copy-done.4
  9.9 0.0 copy-done.5
  9.9 0.0 copy-done
  9.9 0.2 copy.30
  10.1 0.0 copy-done.1
  10.1 0.2 copy.26
  10.3 0.1 iota_compare_fusion
  10.4 0.0 copy-start.2
  10.4 0.7 multiply_reduce_fusion
  11.1 15.5 %collective-permute-done = bf16[512,384]{0,1:T(8,128)(2,1)S(1)} collective-permute-done((bf16[512,384]{0,1:T(8,128)(2,1)S(1)}, bf16[512,384]{0,1:T(8,128)(2,1)S(1)}, u32[]{:S(2)}, u32[]{:S(2)}) %collective-permute-start) | collective-permute-done | bytes 393248 | tf_op jit(solution)/shard_map/ppermute | solution.py:17
  26.6 0.2 fusion.25
  26.8 27.1 %psum.22 = f32[512]{0:T(512)S(1)} all-reduce(f32[512]{0:T(512)S(1)} %get-tuple-element.8), channel_id=1, replica_groups=mesh['section'=48,'tensor'=16] {'tensor'}, use_global_device_ids=true, to_apply=%region_5.6 | all-reduce | flops 512 | bytes 4096 | tf_op jit(solution)/shard_map/psum | solution.py:99
  54.0 0.2 fusion.20
  54.1 2.3 %fusion.53 = f32[3,512,512]{2,1,0:T(8,128)} fusion(bf16[512,3,128]{0,2,1:T(8,128)(2,1)S(1)} %bitcast.77, bf16[512,3,128]{0,2,1:T(8,128)(2,1)S(1)} %bitcast.75), kind=kOutput, calls=%fused_computation.78 | convolution fusion | flops 201326592 | bytes 3932160 | tf_op jit(solution)/shard_map/qhd,khd->hqk/dot_general | solution.py:73
  56.5 0.0 copy-done.2
  56.5 3.0 %fusion.49 = (f32[3,512]{1,0:T(4,128)S(1)}, f32[3,512,512]{1,2,0:T(8,128)}) fusion(pred[512,512]{0,1:T(8,128)(4,1)S(1)} %iota_compare_fusion, bf16[512,3,128]{0,2,1:T(8,128)(2,1)S(1)} %bitcast.80, bf16[512,3,128]{0,2,1:T(8,128)(2,1)S(1)} %bitcast.82), kind=kOutput, calls=%fused_computation.74 | convolution fusion | flops 204472832 | bytes 4200448 | tf_op jit(solution)/shard_map/sub | solution.py:46
  59.5 0.0 copy-start.6
  59.5 0.6 copy-done.6
  60.1 6.1 %fusion.19 = f32[3,128,512]{2,1,0:T(8,128)S(1)} fusion(bf16[512,3,128]{0,2,1:T(8,128)(2,1)S(1)} %bitcast.83, f32[3,512,512]{2,1,0:T(8,128)} %fusion.53, f32[3,512,512]{1,2,0:T(8,128)} %get-tuple-element.18, f32[3,512]{1,0:T(4,128)S(1)} %get-tuple-element.17), kind=kOutput, calls=%fused_computation.27 | convolution fusion | flops 206833664 | bytes 7477248 | tf_op jit(solution)/shard_map/hqk,khd->qhd/dot_general | solution.py:78
  66.2 0.0 copy-start.7
  66.2 6.0 %fusion.18 = f32[3,128,512]{2,1,0:T(8,128)S(1)} fusion(bf16[512,3,128]{0,2,1:T(8,128)(2,1)S(1)} %bitcast.81, f32[3,512,512]{2,1,0:T(8,128)} %fusion.53, f32[3,512,512]{1,2,0:T(8,128)} %get-tuple-element.18, f32[3,512]{1,0:T(4,128)} %copy-done.6), kind=kOutput, calls=%fused_computation.26 | convolution fusion | flops 206833664 | bytes 7477248 | tf_op jit(solution)/shard_map/hqk,qhd->khd/dot_general | solution.py:79
  72.2 0.0 copy-done.7
  72.2 2.5 %fusion.8 = f32[3,512,128]{1,2,0:T(8,128)S(1)} fusion(bf16[512,3,128]{0,2,1:T(8,128)(2,1)S(1)} %bitcast.76, f32[3,512,512]{1,2,0:T(8,128)} %get-tuple-element.18, f32[3,512]{1,0:T(4,128)S(1)} %copy-done.7), kind=kOutput, calls=%fused_computation.15 | convolution fusion | flops 202899456 | bytes 4331520 | tf_op jit(solution)/shard_map/hqk,qhd->khd/dot_general | solution.py:72
  74.7 0.9 fusion.30
  75.6 0.0 copy-start.3
  75.6 27.3 %all-reduce = (f32[512]{0:T(512)S(1)}, f32[512]{0:T(512)S(1)}) all-reduce(f32[512]{0:T(512)} %multiply_reduce_fusion, f32[512]{0:T(512)} %get-tuple-element.6), channel_id=1, replica_groups=mesh['section'=48,'tensor'=16] {'tensor'}, use_global_device_ids=true, to_apply=%region_1.2 | all-reduce | flops 1024 | bytes 8192 | tf_op jit(solution)/shard_map/psum | solution.py:98
  102.8 0.2 fusion.29
  103.1 19.9 %collective-permute-start.1 = (bf16[512,384]{0,1:T(8,128)(2,1)S(1)}, bf16[512,384]{0,1:T(8,128)(2,1)S(1)}, u32[]{:S(2)}, u32[]{:S(2)}) collective-permute-start(bf16[512,384]{0,1:T(8,128)(2,1)S(1)} %fusion.29), channel_id=1, source_target_pairs={{0,752},{16,0},{32,16},{48,32},{64,48},{80,64},{96,80},{112,96},{1... | collective-permute-start | bytes 1179656 | tf_op jit(solution)/shard_map/ppermute | solution.py:17
  123.0 0.7 fusion.33
  123.7 0.0 copy-done.3
  123.7 1.7 %fusion.50 = (f32[3,512]{1,0:T(4,128)S(1)}, f32[3,512,512]{1,2,0:T(8,128)S(1)}) fusion(f32[3,512,512]{1,2,0:T(8,128)S(1)} %fusion.33, pred[512,512]{0,1:T(8,128)(4,1)S(1)} %copy-done.3), kind=kOutput, calls=%fused_computation.75 | output fusion | flops 4719103 | bytes 6559744 | tf_op jit(solution)/shard_map/sub | solution.py:46
  125.5 0.4 fusion.14
  125.9 0.1 fusion.32
  126.0 0.9 copy.41
  126.9 10.4 %collective-permute-done.1 = bf16[512,384]{0,1:T(8,128)(2,1)S(1)} collective-permute-done((bf16[512,384]{0,1:T(8,128)(2,1)S(1)}, bf16[512,384]{0,1:T(8,128)(2,1)S(1)}, u32[]{:S(2)}, u32[]{:S(2)}) %collective-permute-start.1) | collective-permute-done | bytes 393248 | tf_op jit(solution)/shard_map/ppermute | solution.py:17
  137.3 0.9 copy.42
  (4 shorter events, 0.1 us)
Async XLA Ops:
  0.6 9.2 %copy-start.4 = (f32[1,384]{1,0:T(1,128)S(1)}, f32[1,384]{1,0:T(1,128)}, u32[]{:S(2)}) copy-start(f32[1,384]{1,0:T(1,128)} %param.10) | copy-start | bytes 4612
  0.6 9.2 %copy-start.5 = (f32[1,384]{1,0:T(1,128)S(1)}, f32[1,384]{1,0:T(1,128)}, u32[]{:S(2)}) copy-start(f32[1,384]{1,0:T(1,128)} %param.11) | copy-start | bytes 4612
  0.7 9.2 %copy-start = (bf16[1,512,384]{2,1,0:T(8,128)(2,1)S(1)}, bf16[1,512,384]{2,1,0:T(8,128)(2,1)}, u32[]{:S(2)}) copy-start(bf16[1,512,384]{2,1,0:T(8,128)(2,1)} %param.7) | copy-start | bytes 1179652
  0.7 9.4 %copy-start.1 = (bf16[1,512,384]{2,1,0:T(8,128)(2,1)S(1)}, bf16[1,512,384]{2,1,0:T(8,128)(2,1)}, u32[]{:S(2)}) copy-start(bf16[1,512,384]{2,1,0:T(8,128)(2,1)} %param.6) | copy-start | bytes 1179652
  2.1 24.5 %collective-permute-start = (bf16[512,384]{0,1:T(8,128)(2,1)S(1)}, bf16[512,384]{0,1:T(8,128)(2,1)S(1)}, u32[]{:S(2)}, u32[]{:S(2)}) collective-permute-start(bf16[512,384]{0,1:T(8,128)(2,1)S(1)} %bitcast.79), channel_id=1, source_target_pairs={{0,384},{16,400},{32,416},{48,432},{64,448},{80,464},{96,480},{112... | collective-permute-start | bytes 1179656 | tf_op jit(solution)/shard_map/ppermute | solution.py:17
  10.4 46.1 %copy-start.2 = (pred[512,512]{0,1:T(8,128)(4,1)}, pred[512,512]{0,1:T(8,128)(4,1)S(1)}, u32[]{:S(2)}) copy-start(pred[512,512]{0,1:T(8,128)(4,1)S(1)} %iota_compare_fusion) | copy-start | bytes 786436
  59.5 0.6 copy-start.6
  66.2 6.0 %copy-start.7 = (f32[3,512]{1,0:T(4,128)S(1)}, f32[3,512]{1,0:T(4,128)}, u32[]{:S(2)}) copy-start(f32[3,512]{1,0:T(4,128)} %copy-done.6) | copy-start | bytes 18436
  75.6 48.1 %copy-start.3 = (pred[512,512]{0,1:T(8,128)(4,1)S(1)}, pred[512,512]{0,1:T(8,128)(4,1)}, u32[]{:S(2)}) copy-start(pred[512,512]{0,1:T(8,128)(4,1)} %copy-done.2) | copy-start | bytes 786436
  103.1 34.3 %collective-permute-start.1 = (bf16[512,384]{0,1:T(8,128)(2,1)S(1)}, bf16[512,384]{0,1:T(8,128)(2,1)S(1)}, u32[]{:S(2)}, u32[]{:S(2)}) collective-permute-start(bf16[512,384]{0,1:T(8,128)(2,1)S(1)} %fusion.29), channel_id=1, source_target_pairs={{0,752},{16,0},{32,16},{48,32},{64,48},{80,64},{96,80},{112,96},{1... | collective-permute-start | bytes 1179656 | tf_op jit(solution)/shard_map/ppermute | solution.py:17
where the time goes:
time: 139 us; the launch traced here: 138 us
  blocking collectives  54.4 us (39%)
  starting transfers between devices  26.8 us (19%)
  waiting for transfers between devices  25.9 us (19%)
  matrix products  21 us (15%)
  local copies, waits for them, and re-layouts  4.49 us (3%)
  other arithmetic  4.14 us (3%)
  between operations  1.5 us (1%)
    psum x1, blocking collectives, local(): forward_total = lax.psum(local_squares(current), 'tensor')  27.3 us
    psum x1, blocking collectives, local(): recompute_total = lax.psum(local_squares(chosen), 'tensor')  27.1 us
    ppermute x2, starting transfers between devices, passed_along(): return lax.ppermute(x, axis, [(i, (i + by) % size) for i in range(size)])  26.8 us
    ppermute x2, waiting for transfers between devices, passed_along(): return lax.ppermute(x, axis, [(i, (i + by) % size) for i in range(size)])  25.9 us
    dot_general x1, matrix products, backward_terms(): jnp.einsum('hqk,khd->qhd', d_scores, key_heads, preferred_element_type=jn...  6.09 us
    dot_general x1, matrix products, backward_terms(): jnp.einsum('hqk,qhd->khd', d_scores, query_heads, preferred_element_type=...  5.97 us
    unnamed x22, local copies, waits for them, and re-layouts  3.23 us
    sub x1, matrix products, attention_weights(): shifted = scores - jnp.max(scores, axis=-1, keepdims=True)  3.01 us
  transfers between devices with their start and end apart: 2, of which 2 were waited for; matrix products, arithmetic and copies ran while one was open for 4% of the time, Pallas kernels for 0%

commit v1 on v0

v1 whole, which is shorter than its diff:
```python
import functools
import math

import jax
import jax.numpy as jnp
from jax import lax
from jax.experimental import pallas as pl
from jax.experimental.pallas import tpu as pltpu
from jax.sharding import PartitionSpec as P

MESH = pl.DeviceIdType.MESH
HDIM = 128
SEQ = 512
DW = 6144
SECTIONS = 48
PLANES = 12
GROUP = 16
HEADS = 3
BLOCK = 128
LANES = 128
ROWS = SEQ // LANES
CHUNK = 64
CHUNKS = SEQ // CHUNK
EPSILON = 1e-05
SCALE = 1.0 / math.sqrt(HDIM)
EXPONENT = SCALE * math.log2(math.e)
NT = (((1,), (1,)), ((), ()))
TN = (((0,), (0,)), ((), ()))
NN = (((1,), (0,)), ((), ()))


def dot(a, b, dims):
    return lax.dot_general(a, b, dims, preferred_element_type=jnp.float32)


def row_sums(values):
    high = values.astype(jnp.bfloat16)
    low = (values - high.astype(jnp.float32)).astype(jnp.bfloat16)
    ones = jnp.ones((8, values.shape[-1]), jnp.bfloat16)
    return (dot(ones, high, NT) + dot(ones, low, NT))[0:1]


def spread_columns(lane_rows, out_ref):
    for b in range(ROWS):
        block = jnp.broadcast_to(lane_rows[b : b + 1], (LANES, LANES))
        out_ref[pl.ds(b * LANES, LANES), :] = block.T


def block_weights(keys, queries, lo, hi):
    scores = dot(keys[:hi], queries[lo:hi], NT)
    width = hi - lo
    tail = scores[lo:]
    u = lax.broadcasted_iota(jnp.int32, (width, width), 0)
    t = lax.broadcasted_iota(jnp.int32, (width, width), 1)
    tail = jnp.where(u <= t, tail, -1e30)
    scores = tail if lo == 0 else jnp.concatenate([scores[:lo], tail], axis=0)
    top = jnp.max(scores, axis=0, keepdims=True)
    exponent = jnp.exp2((scores - top) * EXPONENT)
    return exponent * (1.0 / jnp.sum(exponent, axis=0, keepdims=True))


def kernel(
    ev_ref, li_ref, g_ref, st_ref, gq_ref, gk_ref,
    lo_ref, out_ref,
    li_v, g_v, own_v, away_v, got_v, x_v, lo_v, dn_v, dk_v, dv_v, dx_v, relay_v,
    part_v, parts_v, extra_v, theirs_v, inner_v, inners_v, f_v, fb_v, cb_v,
    li_s, g_s, own_s, away_s, lo_s,
    stash_ss, stash_rs, sq_ss, sq_rs, ex_ss, ex_rs, in_ss, in_rs,
    dx_ss, dx_rs, rel_rs, fwd_ss,
):
    s, t = lax.axis_index("section"), lax.axis_index("tensor")
    z = lax.rem(s, PLANES)
    first, last = z == 0, z == PLANES - 1

    def section(by):
        return lax.rem(s + (by + SECTIONS), SECTIONS)

    def remote(src, dst, ss, rs, to_s, to_t):
        return pltpu.make_async_remote_copy(
            src_ref=src, dst_ref=dst, send_sem=ss, recv_sem=rs,
            device_id={"section": to_s, "tensor": to_t}, device_id_type=MESH)

    def heads_in(src, dst, sems):
        return [pltpu.make_async_copy(src.at[:, pl.ds(h * HDIM, HDIM)], dst.at[h], sems.at[h]) for h in range(HEADS)]

    away_in = heads_in(st_ref.at[1], away_v, away_s)
    li_in = heads_in(li_ref, li_v, li_s)
    own_in = heads_in(st_ref.at[0], own_v, own_s)
    g_in = heads_in(g_ref, g_v, g_s)
    for c in away_in + li_in + own_in + g_in:
        c.start()

    barrier = pltpu.get_barrier_semaphore()

    def greet(to_s, to_t):
        pl.semaphore_signal(barrier, inc=1, device_id={"section": to_s, "tensor": to_t}, device_id_type=MESH)

    met = (SECTIONS // 2, -1, 1, -PLANES, PLANES, 1 - PLANES, PLANES - 1)
    for by in met:
        greet(section(by), t)
    for by in range(1, GROUP):
        greet(s, lax.rem(t + by, GROUP))

    def squares(ref, slot):
        total = jnp.zeros((1, SEQ), jnp.float32)
        for h in range(HEADS):
            wide = ref[h].astype(jnp.float32)
            total = total + row_sums(wide * wide)
        for b in range(ROWS):
            part_v[pl.ds(slot * ROWS + b, 1), :] = total[:, b * LANES : (b + 1) * LANES]

    for c in away_in:
        c.wait()
    squares(away_v, 2)
    for c in li_in:
        c.wait()
    squares(li_v, 0)
    for c in own_in:
        c.wait()
    squares(own_v, 1)
    for b in range(12, 16):
        part_v[pl.ds(b, 1), :] = jnp.zeros((1, LANES), jnp.float32)

    pl.semaphore_wait(barrier, len(met) + GROUP - 1)

    stash = [remote(away_v.at[h], got_v.at[h], stash_ss.at[h], stash_rs.at[h], section(SECTIONS // 2), t) for h in range(HEADS)]
    shares = [remote(part_v, parts_v.at[i], sq_ss.at[i], sq_rs.at[i], s, lax.rem(t + i, GROUP)) for i in range(1, GROUP)]
    for c in shares:
        c.start()
    for c in stash:
        c.start()
    for c in shares:
        c.wait_recv()
    totals = part_v[...]
    for i in range(1, GROUP):
        totals = totals + parts_v[i]
    extra_v[...] = totals[8:16]
    extra = remote(extra_v, theirs_v, ex_ss, ex_rs, section(SECTIONS // 2), t)
    extra.start()

    def factor_of(total):
        return lax.rsqrt(total / DW + EPSILON)

    spread_columns(factor_of(totals[0:ROWS]), fb_v)
    for c in g_in:
        c.wait()

    def forward(h, carry):
        cols = pl.ds(pl.multiple_of(h * HDIM, HDIM), HDIM)
        wide = li_v[h].astype(jnp.float32)
        normed = wide * fb_v[...]
        queries = (normed * gq_ref[:, cols]).astype(jnp.bfloat16)
        keys = (normed * gk_ref[:, cols]).astype(jnp.bfloat16)
        values = normed.astype(jnp.bfloat16)
        for lo in range(0, SEQ, BLOCK):
            hi = lo + BLOCK
            weights = block_weights(keys, queries, lo, hi).astype(jnp.bfloat16)
            mixed = dot(weights, values[:hi], TN)
            lo_v[h, pl.ds(lo, BLOCK), :] = (wide[lo:hi] + mixed).astype(jnp.bfloat16)
        pltpu.make_async_copy(lo_v.at[h], lo_ref.at[:, cols], lo_s.at[h]).start()
        return carry

    lax.fori_loop(0, HEADS, forward, 0)

    extra.wait_recv()
    evicted = jnp.full((8, LANES), ev_ref[0], jnp.int32) == 1
    own_total = totals[4:8]
    f_v[0:ROWS] = factor_of(jnp.where(evicted[0:ROWS], theirs_v[0:ROWS], own_total))
    spread_columns(f_v[...], fb_v)
    picked = jnp.full((SEQ, HDIM), ev_ref[0], jnp.int32) == 1

    def backward(h, partial):
        cols = pl.ds(pl.multiple_of(h * HDIM, HDIM), HDIM)
        remote(away_v.at[h], got_v.at[h], stash_ss.at[h], stash_rs.at[h], section(SECTIONS // 2), t).wait_recv()
        wide = jnp.where(picked, got_v[h].astype(jnp.float32), own_v[h].astype(jnp.float32))
        x_v[h] = wide.astype(jnp.bfloat16)
        normed = wide * fb_v[...]
        gq, gk = gq_ref[:, cols], gk_ref[:, cols]
        queries = (normed * gq).astype(jnp.bfloat16)
        keys = (normed * gk).astype(jnp.bfloat16)
        values = normed.astype(jnp.bfloat16)
        grads = g_v[h]
        for lo in range(SEQ - BLOCK, -1, -BLOCK):
            hi = lo + BLOCK
            weights = block_weights(keys, queries, lo, hi)
            d_weights = dot(values[:hi], grads[lo:hi], NT)
            delta = jnp.sum(weights * d_weights, axis=0, keepdims=True)
            d_scores = (weights * (d_weights - delta) * SCALE).astype(jnp.bfloat16)
            d_keys = dot(d_scores, queries[lo:hi], NN)
            d_values = dot(weights.astype(jnp.bfloat16), grads[lo:hi], NN)
            if hi == SEQ:
                dk_v[...] = d_keys
                dv_v[...] = d_values
            else:
                dk_v[0:hi] += d_keys
                dv_v[0:hi] += d_values
            dn_v[h, pl.ds(lo, BLOCK), :] = dot(d_scores, keys[:hi], TN) * gq
        d_normed = dn_v[h] + dk_v[...] * gk + dv_v[...]
        dn_v[h] = d_normed
        return partial + row_sums(d_normed * wide)

    partial = lax.fori_loop(0, HEADS, backward, jnp.zeros((1, SEQ), jnp.float32))
    for b in range(ROWS):
        inner_v[pl.ds(b, 1), :] = partial[:, b * LANES : (b + 1) * LANES]
    inner_v[ROWS:8] = jnp.zeros((8 - ROWS, LANES), jnp.float32)
    shares_in = [remote(inner_v, inners_v.at[i], in_ss.at[i], in_rs.at[i], s, lax.rem(t + i, GROUP)) for i in range(1, GROUP)]
    for c in shares_in:
        c.start()
    for c in shares_in:
        c.wait_recv()
    inner = inner_v[...]
    for i in range(1, GROUP):
        inner = inner + inners_v[i]
    f = f_v[...]
    spread_columns(f * f * f * inner[0:ROWS] / DW, cb_v)

    def rows_of(c):
        return pl.ds(pl.multiple_of(c * CHUNK, CHUNK), CHUNK)

    def make(c):
        rows = rows_of(c)
        for h in range(HEADS):
            value = (g_v[h, rows, :].astype(jnp.float32) + fb_v[rows, :] * dn_v[h, rows, :]
                     - x_v[h, rows, :].astype(jnp.float32) * cb_v[rows, :])
            dx_v[rows, h * HDIM : (h + 1) * HDIM] = value.astype(jnp.bfloat16)

    def plain(c):
        return remote(dx_v.at[rows_of(c)], out_ref.at[rows_of(c)], dx_ss.at[c], dx_rs.at[c], section(-1), t)

    def leg(c, by):
        return remote(dx_v.at[rows_of(c)], relay_v.at[rows_of(c)], dx_ss.at[c], rel_rs.at[c], section(by), t)

    def onward(c, by):
        return remote(relay_v.at[rows_of(c)], out_ref.at[rows_of(c)], fwd_ss.at[c], dx_rs.at[c], section(by), t)

    half = CHUNKS // 2

    def loop(start, stop, body):
        def step(c, carry):
            body(c)
            return carry

        lax.fori_loop(start, stop, step, 0)

    @pl.when(jnp.logical_not(first))
    def _():
        def send(c):
            make(c)
            plain(c).start()

        loop(0, CHUNKS, send)

    @pl.when(first)
    def _():
        def send(c):
            make(c)
            leg(c, -PLANES).start()
            make(c + half)
            leg(c + half, PLANES - 1).start()

        def forward_on(c):
            leg(c, -PLANES).wait_recv()
            onward(c, PLANES - 1).start()

        loop(0, half, send)
        loop(0, half, forward_on)
        loop(0, half, lambda c: onward(c, PLANES - 1).wait_send())

    @pl.when(last)
    def _():
        def forward_on(c):
            leg(c, PLANES - 1).wait_recv()
            onward(c, -PLANES).start()

        loop(half, CHUNKS, forward_on)
        loop(half, CHUNKS, lambda c: onward(c, -PLANES).wait_send())

    def finish(c):
        plain(c).wait()

    loop(0, CHUNKS, finish)
    for h in range(HEADS):
        pltpu.make_async_copy(lo_v.at[h], lo_ref.at[:, pl.ds(h * HDIM, HDIM)], lo_s.at[h]).wait()
    for c in stash + shares + shares_in + [extra]:
        c.wait_send()


def local(layer_input, grad_input, stashed, eviction, query_gain, key_gain):
    head_buffer = pltpu.VMEM((HEADS, SEQ, HDIM), jnp.bfloat16)
    column = pltpu.VMEM((SEQ, HDIM), jnp.float32)
    dma = pltpu.SemaphoreType.DMA
    anywhere, vmem = pl.BlockSpec(memory_space=pl.ANY), pl.BlockSpec(memory_space=pltpu.VMEM)
    shape = jax.ShapeDtypeStruct((SEQ, HEADS * HDIM), jnp.bfloat16)
    output, passed = pl.pallas_call(
        kernel,
        out_shape=(shape, shape),
        in_specs=[pl.BlockSpec(memory_space=pltpu.SMEM), anywhere, anywhere, anywhere, vmem, vmem],
        out_specs=(anywhere, anywhere),
        scratch_shapes=[head_buffer] * 7 + [
            pltpu.VMEM((HEADS, SEQ, HDIM), jnp.float32), column, column,
            pltpu.VMEM((SEQ, HEADS * HDIM), jnp.bfloat16), pltpu.VMEM((SEQ, HEADS * HDIM), jnp.bfloat16),
            pltpu.VMEM((16, LANES), jnp.float32), pltpu.VMEM((GROUP, 16, LANES), jnp.float32),
            pltpu.VMEM((8, LANES), jnp.float32), pltpu.VMEM((8, LANES), jnp.float32),
            pltpu.VMEM((8, LANES), jnp.float32), pltpu.VMEM((GROUP, 8, LANES), jnp.float32),
            pltpu.VMEM((ROWS, LANES), jnp.float32), column, column,
        ] + [dma((HEADS,))] * 7 + [dma((GROUP,)), dma((GROUP,)), dma, dma, dma((GROUP,)), dma((GROUP,))]
        + [dma((CHUNKS,))] * 4,
        compiler_params=pltpu.CompilerParams(collective_id=0, has_side_effects=True, vmem_limit_bytes=56 * 2**20),
        name="tick",
    )(eviction, layer_input[0], grad_input[0], stashed[0], query_gain, key_gain)
    return (output[None], passed[None])


def solution(mesh):
    placed = (
        P("section", None, "tensor"),
        P("section", None, "tensor"),
        P("section", None, None, "tensor"),
        P("section"),
        P("section", "tensor"),
        P("section", "tensor"),
    )
    return jax.shard_map(
        local,
        mesh=mesh,
        in_specs=placed,
        out_specs=(P("section", None, "tensor"), P("section", None, "tensor")),
        check_vma=False,
    )
```

time: 139 us -> 67.5 us (0.49)
  the two profiles are of different devices: /device:TPU:8 before, /device:TPU:16 now
where the time goes in v1:
time: 67.5 us; the launch traced here: 67.3 us
  Pallas kernels  63.4 us (94%)
  local copies, waits for them, and re-layouts  2.58 us (4%)
  between operations  1.29 us (2%)
    pallas_call x1, Pallas kernels, local(): pl.pallas_call(kernel, out_shape=(shape, shape), in_specs=[pl.BlockSpec(m...  63.4 us
    unnamed x4, local copies, waits for them, and re-layouts  2.58 us

profile of v1, /device:TPU:16, one launch (start us, length us, event | category | flops | bytes accessed | tf_op | source)
XLA Modules:
  0.0 67.3 jit_solution(8029886098189876260)
XLA Ops:
  1.3 63.4 %tick.1 = (bf16[512,384]{1,0:T(8,128)(2,1)}, bf16[512,384]{1,0:T(8,128)(2,1)}) custom-call(s32[1]{0:T(128)S(6)} %copy.10.ev_ref, bf16[512,384]{1,0:T(8,128)(2,1)} %bitcast.8, bf16[512,384]{1,0:T(8,128)(2,1)} %bitcast.9, bf16[2,512,384]{2,1,0:T(8,128)(2,1)} %bitcast.5, f32[1,384]{1,0:T(1,128)} %gq_ref.1, f32[1,384]{1,0:T(1,128)} %gk_ref.1), custom_call_target="tpu_custom_call" | custom-call | tf_op jit(solution)/shard_map/tick/pallas_call | solution.py:294
  64.7 0.0 copy-start
  64.7 1.8 %copy.11 = bf16[1,512,384]{2,1,0:T(8,128)(2,1)} copy(bf16[1,512,384]{2,1,0:T(8,128)(2,1)} %bitcast.7) | data formatting | bytes 786432
  66.6 0.0 copy-done
  66.6 0.7 %copy.12 = bf16[1,512,384]{2,1,0:T(8,128)(2,1)} copy(bf16[1,512,384]{2,1,0:T(8,128)(2,1)S(1)} %bitcast.6) | data formatting | bytes 786432
Async XLA Ops:
  64.7 1.8 %copy-start = (bf16[512,384]{1,0:T(8,128)(2,1)S(1)}, bf16[512,384]{1,0:T(8,128)(2,1)}, u32[]{:S(2)}) copy-start(bf16[512,384]{1,0:T(8,128)(2,1)} %get-tuple-element.5) | copy-start | bytes 1179652

commit v2 on v1

--- a/solution.py
+++ b/solution.py
@@ -61,16 +61,17 @@
 
 def kernel(
     ev_ref, li_ref, g_ref, st_ref, gq_ref, gk_ref,
-    lo_ref, out_ref,
-    li_v, g_v, own_v, away_v, got_v, x_v, lo_v, dn_v, dk_v, dv_v, dx_v, relay_v,
-    part_v, parts_v, extra_v, theirs_v, inner_v, inners_v, f_v, fb_v, cb_v,
-    li_s, g_s, own_s, away_s, lo_s,
-    stash_ss, stash_rs, sq_ss, sq_rs, ex_ss, ex_rs, in_ss, in_rs,
+    lo_ref, a_ref, x_ref, c_ref,
+    ev_v, gq_v, gk_v, li_v, g_v, own_v, away_v, got_v, x_v, a_v, lo_v, dn_v, dk_v, dv_v, dx_v, relay_v,
+    part_v, parts_v, extra_v, theirs_v, inner_v, inners_v, f_v, c_v, fb_v, cb_v,
+    ready, small_s, li_s, g_s, own_s, away_s, lo_s,
+    stash_ss, stash_rs, a_ss, a_rs, x_ss, x_rs, sq_ss, sq_rs, in_ss, in_rs, ex_ss, ex_rs, c_ss, c_rs,
     dx_ss, dx_rs, rel_rs, fwd_ss,
 ):
     s, t = lax.axis_index("section"), lax.axis_index("tensor")
     z = lax.rem(s, PLANES)
     first, last = z == 0, z == PLANES - 1
+    inland = jnp.logical_not(first)
 
     def section(by):
         return lax.rem(s + (by + SECTIONS), SECTIONS)
@@ -80,6 +81,25 @@
             src_ref=src, dst_ref=dst, send_sem=ss, recv_sem=rs,
             device_id={"section": to_s, "tensor": to_t}, device_id_type=MESH)
 
+    barrier = pltpu.get_barrier_semaphore()
+
+    def greet(to_s, to_t, semaphore=barrier):
+        pl.semaphore_signal(semaphore, inc=1, device_id={"section": to_s, "tensor": to_t}, device_id_type=MESH)
+
+    met = (SECTIONS // 2, -PLANES, PLANES)
+    for by in met:
+        greet(section(by), t)
+    for by in range(1, GROUP):
+        greet(s, lax.rem(t + by, GROUP))
+
+    @pl.when(z >= 2)
+    def _():
+        greet(section(-1), t)
+
+    @pl.when(jnp.logical_and(inland, jnp.logical_not(last)))
+    def _():
+        greet(section(1), t)
+
     def heads_in(src, dst, sems):
         return [pltpu.make_async_copy(src.at[:, pl.ds(h * HDIM, HDIM)], dst.at[h], sems.at[h]) for h in range(HEADS)]
 
@@ -87,19 +107,31 @@
     li_in = heads_in(li_ref, li_v, li_s)
     own_in = heads_in(st_ref.at[0], own_v, own_s)
     g_in = heads_in(g_ref, g_v, g_s)
-    for c in away_in + li_in + own_in + g_in:
+    small_in = [
+        pltpu.make_async_copy(ev_ref, ev_v, small_s.at[0]),
+        pltpu.make_async_copy(gq_ref, gq_v, small_s.at[1]),
+        pltpu.make_async_copy(gk_ref, gk_v, small_s.at[2]),
+    ]
+    for c in away_in + li_in + own_in + small_in + g_in:
         c.start()
 
-    barrier = pltpu.get_barrier_semaphore()
-
-    def greet(to_s, to_t):
-        pl.semaphore_signal(barrier, inc=1, device_id={"section": to_s, "tensor": to_t}, device_id_type=MESH)
-
-    met = (SECTIONS // 2, -1, 1, -PLANES, PLANES, 1 - PLANES, PLANES - 1)
-    for by in met:
-        greet(section(by), t)
-    for by in range(1, GROUP):
-        greet(s, lax.rem(t + by, GROUP))
+    near = len(met) + GROUP - 1
+    away_in[0].wait()
+    pl.semaphore_wait(barrier, jnp.where(first, near, near + 2))
+
+    @pl.when(first)
+    def _():
+        greet(section(1), t)
+        greet(section(PLANES - 1), t)
+
+    @pl.when(last)
+    def _():
+        greet(section(1 - PLANES), t, ready)
+
+    def stash(h):
+        return remote(away_v.at[h], got_v.at[h], stash_ss.at[h], stash_rs.at[h], section(SECTIONS // 2), t)
+
+    stash(0).start()
 
     def squares(ref, slot):
         total = jnp.zeros((1, SEQ), jnp.float32)
@@ -109,7 +141,7 @@
         for b in range(ROWS):
             part_v[pl.ds(slot * ROWS + b, 1), :] = total[:, b * LANES : (b + 1) * LANES]
 
-    for c in away_in:
+    for c in away_in[1:]:
         c.wait()
     squares(away_v, 2)
     for c in li_in:
@@ -118,17 +150,14 @@
     for c in own_in:
         c.wait()
     squares(own_v, 1)
-    for b in range(12, 16):
-        part_v[pl.ds(b, 1), :] = jnp.zeros((1, LANES), jnp.float32)
-
-    pl.semaphore_wait(barrier, len(met) + GROUP - 1)
-
-    stash = [remote(away_v.at[h], got_v.at[h], stash_ss.at[h], stash_rs.at[h], section(SECTIONS // 2), t) for h in range(HEADS)]
+    part_v[12:16] = jnp.zeros((4, LANES), jnp.float32)
+
     shares = [remote(part_v, parts_v.at[i], sq_ss.at[i], sq_rs.at[i], s, lax.rem(t + i, GROUP)) for i in range(1, GROUP)]
     for c in shares:
         c.start()
-    for c in stash:
-        c.start()
+    stash(1).start()
+    for c in small_in + g_in:
+        c.wait()
     for c in shares:
         c.wait_recv()
     totals = part_v[...]
@@ -137,20 +166,19 @@
     extra_v[...] = totals[8:16]
     extra = remote(extra_v, theirs_v, ex_ss, ex_rs, section(SECTIONS // 2), t)
     extra.start()
+    stash(2).start()
 
     def factor_of(total):
         return lax.rsqrt(total / DW + EPSILON)
 
     spread_columns(factor_of(totals[0:ROWS]), fb_v)
-    for c in g_in:
-        c.wait()
 
     def forward(h, carry):
         cols = pl.ds(pl.multiple_of(h * HDIM, HDIM), HDIM)
         wide = li_v[h].astype(jnp.float32)
         normed = wide * fb_v[...]
-        queries = (normed * gq_ref[:, cols]).astype(jnp.bfloat16)
-        keys = (normed * gk_ref[:, cols]).astype(jnp.bfloat16)
+        queries = (normed * gq_v[:, cols]).astype(jnp.bfloat16)
+        keys = (normed * gk_v[:, cols]).astype(jnp.bfloat16)
         values = normed.astype(jnp.bfloat16)
         for lo in range(0, SEQ, BLOCK):
             hi = lo + BLOCK
@@ -163,19 +191,29 @@
     lax.fori_loop(0, HEADS, forward, 0)
 
     extra.wait_recv()
-    evicted = jnp.full((8, LANES), ev_ref[0], jnp.int32) == 1
-    own_total = totals[4:8]
-    f_v[0:ROWS] = factor_of(jnp.where(evicted[0:ROWS], theirs_v[0:ROWS], own_total))
+    evicted = jnp.full((ROWS, LANES), ev_v[0], jnp.int32) == 1
+    f_v[...] = factor_of(jnp.where(evicted, theirs_v[0:ROWS], totals[4:8]))
     spread_columns(f_v[...], fb_v)
-    picked = jnp.full((SEQ, HDIM), ev_ref[0], jnp.int32) == 1
+    picked = jnp.full((SEQ, HDIM), ev_v[0], jnp.int32) == 1
+
+    def send_x(h):
+        return remote(x_v.at[h], x_ref.at[h], x_ss.at[h], x_rs.at[h], section(-1), t)
+
+    def send_a(h):
+        return remote(a_v.at[h], a_ref.at[h], a_ss.at[h], a_rs.at[h], section(-1), t)
 
     def backward(h, partial):
         cols = pl.ds(pl.multiple_of(h * HDIM, HDIM), HDIM)
-        remote(away_v.at[h], got_v.at[h], stash_ss.at[h], stash_rs.at[h], section(SECTIONS // 2), t).wait_recv()
+        stash(h).wait_recv()
         wide = jnp.where(picked, got_v[h].astype(jnp.float32), own_v[h].astype(jnp.float32))
         x_v[h] = wide.astype(jnp.bfloat16)
+
+        @pl.when(inland)
+        def _():
+            send_x(h).start()
+
         normed = wide * fb_v[...]
-        gq, gk = gq_ref[:, cols], gk_ref[:, cols]
+        gq, gk = gq_v[:, cols], gk_v[:, cols]
         queries = (normed * gq).astype(jnp.bfloat16)
         keys = (normed * gk).astype(jnp.bfloat16)
         values = normed.astype(jnp.bfloat16)
@@ -197,6 +235,12 @@
             dn_v[h, pl.ds(lo, BLOCK), :] = dot(d_scores, keys[:hi], TN) * gq
         d_normed = dn_v[h] + dk_v[...] * gk + dv_v[...]
         dn_v[h] = d_normed
+        a_v[h] = (grads.astype(jnp.float32) + fb_v[...] * d_normed).astype(jnp.bfloat16)
+
+        @pl.when(inland)
+        def _():
+            send_a(h).start()
+
         return partial + row_sums(d_normed * wide)
 
     partial = lax.fori_loop(0, HEADS, backward, jnp.zeros((1, SEQ), jnp.float32))
@@ -212,26 +256,30 @@
     for i in range(1, GROUP):
         inner = inner + inners_v[i]
     f = f_v[...]
-    spread_columns(f * f * f * inner[0:ROWS] / DW, cb_v)
-
-    def rows_of(c):
-        return pl.ds(pl.multiple_of(c * CHUNK, CHUNK), CHUNK)
+    scalars = f * f * f * inner[0:ROWS] / DW
+    c_v[0:ROWS] = scalars
+    c_v[ROWS:8] = jnp.zeros((8 - ROWS, LANES), jnp.float32)
+    send_c = remote(c_v, c_ref, c_ss, c_rs, section(-1), t)
+
+    @pl.when(inland)
+    def _():
+        send_c.start()
+
+    def part(ref, c):
+        return ref.at[:, pl.ds(pl.multiple_of(c * CHUNK, CHUNK), CHUNK)]
 
     def make(c):
-        rows = rows_of(c)
+        rows = pl.ds(pl.multiple_of(c * CHUNK, CHUNK), CHUNK)
         for h in range(HEADS):
             value = (g_v[h, rows, :].astype(jnp.float32) + fb_v[rows, :] * dn_v[h, rows, :]
                      - x_v[h, rows, :].astype(jnp.float32) * cb_v[rows, :])
-            dx_v[rows, h * HDIM : (h + 1) * HDIM] = value.astype(jnp.bfloat16)
-
-    def plain(c):
-        return remote(dx_v.at[rows_of(c)], out_ref.at[rows_of(c)], dx_ss.at[c], dx_rs.at[c], section(-1), t)
+            dx_v[h, rows, :] = value.astype(jnp.bfloat16)
 
     def leg(c, by):
-        return remote(dx_v.at[rows_of(c)], relay_v.at[rows_of(c)], dx_ss.at[c], rel_rs.at[c], section(by), t)
+        return remote(part(dx_v, c), part(relay_v, c), dx_ss.at[c], rel_rs.at[c], section(by), t)
 
     def onward(c, by):
-        return remote(relay_v.at[rows_of(c)], out_ref.at[rows_of(c)], fwd_ss.at[c], dx_rs.at[c], section(by), t)
+        return remote(part(relay_v, c), part(a_ref, c), fwd_ss.at[c], dx_rs.at[c], section(by), t)
 
     half = CHUNKS // 2
 
@@ -242,16 +290,11 @@
 
         lax.fori_loop(start, stop, step, 0)
 
-    @pl.when(jnp.logical_not(first))
-    def _():
-        def send(c):
-            make(c)
-            plain(c).start()
-
-        loop(0, CHUNKS, send)
-
     @pl.when(first)
     def _():
+        spread_columns(scalars, cb_v)
+        pl.semaphore_wait(ready, 1)
+
         def send(c):
             make(c)
             leg(c, -PLANES).start()
@@ -265,6 +308,7 @@
         loop(0, half, send)
         loop(0, half, forward_on)
         loop(0, half, lambda c: onward(c, PLANES - 1).wait_send())
+        loop(0, CHUNKS, lambda c: leg(c, -PLANES).wait_send())
 
     @pl.when(last)
     def _():
@@ -274,40 +318,77 @@
 
         loop(half, CHUNKS, forward_on)
         loop(half, CHUNKS, lambda c: onward(c, -PLANES).wait_send())
-
-    def finish(c):
-        plain(c).wait()
-
-    loop(0, CHUNKS, finish)
+        loop(0, CHUNKS, lambda c: onward(c, -PLANES).wait_recv())
+
+    @pl.when(inland)
+    def _():
+        for h in range(HEADS):
+            send_x(h).wait_send()
+            send_a(h).wait_send()
+        send_c.wait_send()
+
     for h in range(HEADS):
         pltpu.make_async_copy(lo_v.at[h], lo_ref.at[:, pl.ds(h * HDIM, HDIM)], lo_s.at[h]).wait()
-    for c in stash + shares + shares_in + [extra]:
+        stash(h).wait_send()
+    for c in shares + shares_in + [extra]:
         c.wait_send()
+
+    @pl.when(jnp.logical_not(last))
+    def _():
+        for h in range(HEADS):
+            send_x(h).wait_recv()
+            send_a(h).wait_recv()
+        send_c.wait_recv()
+
+
+def finish(lo_ref, a_ref, x_ref, c_ref, out_ref, grad_ref, cb_v):
+    last = lax.rem(lax.axis_index("section"), PLANES) == PLANES - 1
+    out_ref[...] = lo_ref[...]
+
+    @pl.when(last)
+    def _():
+        for h in range(HEADS):
+            grad_ref[:, h * HDIM : (h + 1) * HDIM] = a_ref[h]
+
+    @pl.when(jnp.logical_not(last))
+    def _():
+        spread_columns(c_ref[...], cb_v)
+        for h in range(HEADS):
+            value = a_ref[h].astype(jnp.float32) - x_ref[h].astype(jnp.float32) * cb_v[...]
+            grad_ref[:, h * HDIM : (h + 1) * HDIM] = value.astype(jnp.bfloat16)
 
 
 def local(layer_input, grad_input, stashed, eviction, query_gain, key_gain):
     head_buffer = pltpu.VMEM((HEADS, SEQ, HDIM), jnp.bfloat16)
     column = pltpu.VMEM((SEQ, HDIM), jnp.float32)
+    gain = pltpu.VMEM((1, HEADS * HDIM), jnp.float32)
+    tile = pltpu.VMEM((8, LANES), jnp.float32)
     dma = pltpu.SemaphoreType.DMA
     anywhere, vmem = pl.BlockSpec(memory_space=pl.ANY), pl.BlockSpec(memory_space=pltpu.VMEM)
-    shape = jax.ShapeDtypeStruct((SEQ, HEADS * HDIM), jnp.bfloat16)
-    output, passed = pl.pallas_call(
+    flat = jax.ShapeDtypeStruct((SEQ, HEADS * HDIM), jnp.bfloat16)
+    split = jax.ShapeDtypeStruct((HEADS, SEQ, HDIM), jnp.bfloat16)
+    lo, a, x, c = pl.pallas_call(
         kernel,
-        out_shape=(shape, shape),
-        in_specs=[pl.BlockSpec(memory_space=pltpu.SMEM), anywhere, anywhere, anywhere, vmem, vmem],
-        out_specs=(anywhere, anywhere),
-        scratch_shapes=[head_buffer] * 7 + [
-            pltpu.VMEM((HEADS, SEQ, HDIM), jnp.float32), column, column,
-            pltpu.VMEM((SEQ, HEADS * HDIM), jnp.bfloat16), pltpu.VMEM((SEQ, HEADS * HDIM), jnp.bfloat16),
+        out_shape=(flat, split, split, jax.ShapeDtypeStruct((8, LANES), jnp.float32)),
+        in_specs=[anywhere] * 6,
+        out_specs=(anywhere,) * 4,
+        scratch_shapes=[pltpu.SMEM((1,), jnp.int32), gain, gain] + [head_buffer] * 8 + [
+            pltpu.VMEM((HEADS, SEQ, HDIM), jnp.float32), column, column, head_buffer, head_buffer,
             pltpu.VMEM((16, LANES), jnp.float32), pltpu.VMEM((GROUP, 16, LANES), jnp.float32),
-            pltpu.VMEM((8, LANES), jnp.float32), pltpu.VMEM((8, LANES), jnp.float32),
-            pltpu.VMEM((8, LANES), jnp.float32), pltpu.VMEM((GROUP, 8, LANES), jnp.float32),
-            pltpu.VMEM((ROWS, LANES), jnp.float32), column, column,
-        ] + [dma((HEADS,))] * 7 + [dma((GROUP,)), dma((GROUP,)), dma, dma, dma((GROUP,)), dma((GROUP,))]
-        + [dma((CHUNKS,))] * 4,
+            tile, tile, tile, pltpu.VMEM((GROUP, 8, LANES), jnp.float32),
+            pltpu.VMEM((ROWS, LANES), jnp.float32), tile, column, column, pltpu.SemaphoreType.REGULAR,
+        ] + [dma((HEADS,))] * 12 + [dma((GROUP,))] * 4 + [dma] * 4 + [dma((CHUNKS,))] * 4,
         compiler_params=pltpu.CompilerParams(collective_id=0, has_side_effects=True, vmem_limit_bytes=56 * 2**20),
         name="tick",
     )(eviction, layer_input[0], grad_input[0], stashed[0], query_gain, key_gain)
+    output, passed = pl.pallas_call(
+        finish,
+        out_shape=(flat, flat),
+        in_specs=[vmem] * 4,
+        out_specs=(vmem, vmem),
+        scratch_shapes=[column],
+        name="finish",
+    )(lo, a, x, c)
     return (output[None], passed[None])
 
 

time: 67.5 us -> 56.8 us (0.84)
  Pallas kernels: 63.4 us -> 55.3 us
  local copies, waits for them, and re-layouts: 2.58 us -> 0 us
    pallas_call x1 -> x2, Pallas kernels: 63.4 us -> 55.3 us  [the longest x1 52.9 us: local(): pl.pallas_call(kernel, out_shape=(flat, split, split, jax.ShapeDtypeStruc...]
    unnamed x4 -> x0, local copies, waits for them, and re-layouts: 2.58 us -> none
where the time goes in v2:
time: 56.8 us; the launch traced here: 56.6 us
  Pallas kernels  55.3 us (97%)
  between operations  1.28 us (2%)
    pallas_call x1, Pallas kernels, local(): pl.pallas_call(kernel, out_shape=(flat, split, split, jax.ShapeDtypeStruc...  52.9 us
    pallas_call x1, Pallas kernels, local(): pl.pallas_call(finish, out_shape=(flat, flat), in_specs=[vmem] * 4, out_s...  2.35 us

profile of v2, /device:TPU:16, one launch (start us, length us, event | category | flops | bytes accessed | tf_op | source)
XLA Modules:
  0.0 56.6 jit_solution(14027155375366699358)
XLA Ops:
  1.3 52.9 %tick.1 = (bf16[512,384]{1,0:T(8,128)(2,1)}, bf16[3,512,128]{2,1,0:T(8,128)(2,1)}, bf16[3,512,128]{2,1,0:T(8,128)(2,1)}, f32[8,128]{1,0:T(8,128)}) custom-call(s32[1]{0:T(128)S(6)} %copy.8.ev_ref, bf16[512,384]{1,0:T(8,128)(2,1)} %bitcast.6, bf16[512,384]{1,0:T(8,128)(2,1)} %bitcast.7, bf16[2,512,384]{2,1,0:T(8,128)(2,1)} %bitcast.5, f32[1,384]{1,0:T(1,128)} %gq_ref.1, ...), custom_call_target="tpu_custom_call" | custom-call | tf_op jit(solution)/shard_map/tick/pallas_call | solution.py:370
  54.2 2.3 %finish.1 = (bf16[512,384]{1,0:T(8,128)(2,1)}, bf16[512,384]{1,0:T(8,128)(2,1)}) custom-call(bf16[512,384]{1,0:T(8,128)(2,1)} %get-tuple-element.8.lo_ref, bf16[3,512,128]{2,1,0:T(8,128)(2,1)} %get-tuple-element.9.a_ref, bf16[3,512,128]{2,1,0:T(8,128)(2,1)} %get-tuple-element.10.x_ref, f32[8,128]{1,0:T(8,128)} %get-tuple-element.11.c_ref), custom_call_target="tpu_custom_call" | custom-call | tf_op jit(solution)/shard_map/finish/pallas_call | solution.py:384

commit v3 on v2

v3 whole, which is shorter than its diff:
```python
import functools
import math

import jax
import jax.numpy as jnp
from jax import lax
from jax.experimental import pallas as pl
from jax.experimental.pallas import tpu as pltpu
from jax.sharding import PartitionSpec as P

MESH = pl.DeviceIdType.MESH
HDIM = 128
SEQ = 512
DW = 6144
SECTIONS = 48
PLANES = 12
GROUP = 16
HEADS = 3
BLOCK = 128
LANES = 128
ROWS = SEQ // LANES
CHUNK = 64
HALF = SEQ // 2
CHUNKS = HALF // CHUNK
EPSILON = 1e-05
SCALE = 1.0 / math.sqrt(HDIM)
EXPONENT = SCALE * math.log2(math.e)
NT = (((1,), (1,)), ((), ()))
TN = (((0,), (0,)), ((), ()))
NN = (((1,), (0,)), ((), ()))


def dot(a, b, dims):
    return lax.dot_general(a, b, dims, preferred_element_type=jnp.float32)


def row_sums(values):
    high = values.astype(jnp.bfloat16)
    low = (values - high.astype(jnp.float32)).astype(jnp.bfloat16)
    ones = jnp.ones((8, values.shape[-1]), jnp.bfloat16)
    return (dot(ones, high, NT) + dot(ones, low, NT))[0:1]


def spread_columns(row, out_ref):
    for lo in range(0, row.shape[1], LANES):
        block = jnp.broadcast_to(row[:, lo : lo + LANES], (LANES, LANES))
        out_ref[pl.ds(lo, LANES), :] = block.T


def one_row(rows):
    return jnp.concatenate([rows[b : b + 1] for b in range(ROWS)], axis=1)


def block_weights(keys, queries, lo, hi):
    scores = dot(keys[:hi], queries[lo:hi], NT)
    width = hi - lo
    tail = scores[lo:]
    u = lax.broadcasted_iota(jnp.int32, (width, width), 0)
    t = lax.broadcasted_iota(jnp.int32, (width, width), 1)
    tail = jnp.where(u <= t, tail, -1e30)
    scores = tail if lo == 0 else jnp.concatenate([scores[:lo], tail], axis=0)
    top = jnp.max(scores, axis=0, keepdims=True)
    exponent = jnp.exp2((scores - top) * EXPONENT)
    return exponent * (1.0 / jnp.sum(exponent, axis=0, keepdims=True))


def kernel(
    ev_ref, li_ref, g_ref, st_ref, gq_ref, gk_ref,
    lo_ref, a_ref, x_ref, c_ref,
    gq_v, gk_v, li_v, g_v, own_v, away_v, got_v, x_v, a_v, lo_v, dq_v, dk_v, dv_v, dx_v, hop_v, rx_v, ra_v, rc_v,
    part_v, parts_v, extra_v, theirs_v, inner_v, fb_v, cb_v,
    ready, opened, small_s, li_s, g_s, own_s, away_s, lo_s,
    stash_ss, stash_rs, a_ss, a_rs, x_ss, x_rs, wa_rs, wx_rs, sq_ss, sq_rs, c_ss, c_rs, wc_rs, ex_ss, ex_rs,
    wa_ss, wx_ss, wc_ss, dx_ss, hop_ss, hop_rs, dx_rs,
):
    s, t = lax.axis_index("section"), lax.axis_index("tensor")
    z = lax.rem(s, PLANES)
    first, last = z == 0, z == PLANES - 1
    inland = jnp.logical_not(first)

    def section(by):
        return lax.rem(s + (by + SECTIONS), SECTIONS)

    def remote(src, dst, ss, rs, to_s, to_t):
        return pltpu.make_async_remote_copy(
            src_ref=src, dst_ref=dst, send_sem=ss, recv_sem=rs,
            device_id={"section": to_s, "tensor": to_t}, device_id_type=MESH)

    barrier = pltpu.get_barrier_semaphore()

    def greet(to_s, to_t, semaphore=barrier):
        pl.semaphore_signal(semaphore, inc=1, device_id={"section": to_s, "tensor": to_t}, device_id_type=MESH)

    second, porter = z == 1, z >= PLANES - 2
    outer = z == PLANES - 2
    greet(section(SECTIONS // 2), t)
    for by in range(1, GROUP):
        greet(s, lax.rem(t + by, GROUP))

    def greet_plane(by, semaphore=barrier):
        for to_t in range(GROUP):
            greet(section(by), to_t, semaphore)

    @pl.when(jnp.logical_and(inland, jnp.logical_not(last)))
    def _():
        greet_plane(1)

    @pl.when(second)
    def _():
        greet_plane(-1)

    @pl.when(first)
    def _():
        greet_plane(PLANES - 1)
        greet_plane(PLANES - 2)

    @pl.when(porter)
    def _():
        greet(section(PLANES), t)

    @pl.when(last)
    def _():
        greet(section(-1), t)

    def heads_in(src, dst, sems):
        return [pltpu.make_async_copy(src.at[:, pl.ds(h * HDIM, HDIM)], dst.at[h], sems.at[h]) for h in range(HEADS)]

    away_in = heads_in(st_ref.at[1], away_v, away_s)
    li_in = heads_in(li_ref, li_v, li_s)
    own_in = heads_in(st_ref.at[0], own_v, own_s)
    g_in = heads_in(g_ref, g_v, g_s)
    small_in = [
        pltpu.make_async_copy(gq_ref, gq_v, small_s.at[1]),
        pltpu.make_async_copy(gk_ref, gk_v, small_s.at[2]),
    ]
    for c in away_in + li_in + own_in + small_in + g_in:
        c.start()

    def count(condition):
        return condition.astype(jnp.int32)

    @pl.when(porter)
    def _():
        pl.semaphore_wait(barrier, 3 * GROUP + 1 + count(outer))
        for to_t in range(GROUP):
            greet(lax.rem(s - z + SECTIONS, SECTIONS), to_t, ready)

    def squares(ref, slot):
        total = jnp.zeros((1, SEQ), jnp.float32)
        for h in range(HEADS):
            wide = ref[h].astype(jnp.float32)
            total = total + row_sums(wide * wide)
        for b in range(ROWS):
            part_v[pl.ds(slot * ROWS + b, 1), :] = total[:, b * LANES : (b + 1) * LANES]

    for c in away_in:
        c.wait()
    squares(away_v, 2)
    for c in li_in:
        c.wait()
    squares(li_v, 0)
    for c in own_in:
        c.wait()
    squares(own_v, 1)
    part_v[12:16] = jnp.zeros((4, LANES), jnp.float32)

    @pl.when(jnp.logical_not(porter))
    def _():
        pl.semaphore_wait(barrier, GROUP + GROUP * count(z != 1))

    @pl.when(first)
    def _():
        greet_plane(1, opened)

    def stash(h):
        return remote(away_v.at[h], got_v.at[h], stash_ss.at[h], stash_rs.at[h], section(SECTIONS // 2), t)

    shares = [remote(part_v, parts_v.at[i], sq_ss.at[i], sq_rs.at[i], s, lax.rem(t + i, GROUP)) for i in range(1, GROUP)]
    for c in shares:
        c.start()
    stash(0).start()
    for c in small_in + g_in:
        c.wait()
    for c in shares:
        c.wait_recv()
    totals = part_v[...]
    for i in range(1, GROUP):
        totals = totals + parts_v[i]
    extra_v[...] = totals[8:16]
    extra = remote(extra_v, theirs_v, ex_ss, ex_rs, section(SECTIONS // 2), t)
    extra.start()
    stash(1).start()
    stash(2).start()

    def factor_of(total):
        return lax.rsqrt(total / DW + EPSILON)

    spread_columns(factor_of(one_row(totals[0:ROWS])), fb_v)

    def forward(h, carry):
        cols = pl.ds(pl.multiple_of(h * HDIM, HDIM), HDIM)
        wide = li_v[h].astype(jnp.float32)
        normed = wide * fb_v[...]
        queries = (normed * gq_v[:, cols]).astype(jnp.bfloat16)
        keys = (normed * gk_v[:, cols]).astype(jnp.bfloat16)
        values = normed.astype(jnp.bfloat16)
        for lo in range(0, SEQ, BLOCK):
            hi = lo + BLOCK
            weights = block_weights(keys, queries, lo, hi).astype(jnp.bfloat16)
            mixed = dot(weights, values[:hi], TN)
            lo_v[h, pl.ds(lo, BLOCK), :] = (wide[lo:hi] + mixed).astype(jnp.bfloat16)
        pltpu.make_async_copy(lo_v.at[h], lo_ref.at[h], lo_s.at[h]).start()
        return carry

    lax.fori_loop(0, HEADS, forward, 0)

    picked = jnp.full((SEQ, HDIM), ev_ref[0], jnp.int32) == 1

    def send_x(h):
        return remote(x_v.at[h], x_ref.at[h], x_ss.at[h], x_rs.at[h], section(-1), t)

    def send_a(h):
        return remote(a_v.at[h], a_ref.at[h], a_ss.at[h], a_rs.at[h], section(-1), t)

    def wrap_x(h, k):
        rows = pl.ds(k * HALF, HALF)
        return remote(x_v.at[h, rows], rx_v.at[h], wx_ss.at[k, h], wx_rs.at[h], section(PLANES - 1 - k), t)

    def wrap_a(h, k):
        rows = pl.ds(k * HALF, HALF)
        return remote(a_v.at[h, rows], ra_v.at[h], wa_ss.at[k, h], wa_rs.at[h], section(PLANES - 1 - k), t)

    def send_c(i):
        return remote(inner_v, c_ref.at[i], c_ss.at[i], c_rs.at[i], section(-1), lax.rem(t + i, GROUP))

    def wrap_c(i, k):
        tokens = pl.ds(k * HALF, HALF)
        return remote(inner_v.at[:, tokens], rc_v.at[i], wc_ss.at[k, i], wc_rs.at[i], section(PLANES - 1 - k), lax.rem(t + i, GROUP))

    def pass_on(whole, halves, h):
        @pl.when(inland)
        def _():
            whole(h).start()

        @pl.when(first)
        def _():
            halves(h, 0).start()
            halves(h, 1).start()

    def choose(h):
        stash(h).wait_recv()
        wide = jnp.where(picked, got_v[h].astype(jnp.float32), own_v[h].astype(jnp.float32))
        x_v[h] = wide.astype(jnp.bfloat16)
        pass_on(send_x, wrap_x, h)

    @pl.when(second)
    def _():
        pl.semaphore_wait(opened, GROUP)

    @pl.when(first)
    def _():
        pl.semaphore_wait(ready, 2 * GROUP)

    choose(0)
    extra.wait_recv()
    evicted = jnp.full((1, SEQ), ev_ref[0], jnp.int32) == 1
    f = factor_of(jnp.where(evicted, one_row(theirs_v[0:ROWS]), one_row(totals[4:8])))
    spread_columns(f, fb_v)

    def backward(h, partial):
        cols = pl.ds(pl.multiple_of(h * HDIM, HDIM), HDIM)
        wide = x_v[h].astype(jnp.float32)
        normed = wide * fb_v[...]
        gq, gk = gq_v[:, cols], gk_v[:, cols]
        queries = (normed * gq).astype(jnp.bfloat16)
        keys = (normed * gk).astype(jnp.bfloat16)
        values = normed.astype(jnp.bfloat16)
        grads = g_v[h]
        for lo in range(SEQ - BLOCK, -1, -BLOCK):
            hi = lo + BLOCK
            weights = block_weights(keys, queries, lo, hi)
            d_weights = dot(values[:hi], grads[lo:hi], NT)
            delta = jnp.sum(weights * d_weights, axis=0, keepdims=True)
            d_scores = (weights * (d_weights - delta) * SCALE).astype(jnp.bfloat16)
            d_keys = dot(d_scores, queries[lo:hi], NN)
            d_values = dot(weights.astype(jnp.bfloat16), grads[lo:hi], NN)
            if hi == SEQ:
                dk_v[...] = d_keys
                dv_v[...] = d_values
            else:
                dk_v[0:hi] += d_keys
                dv_v[0:hi] += d_values
            dq_v[pl.ds(lo, BLOCK), :] = dot(d_scores, keys[:hi], TN) * gq
        d_normed = dq_v[...] + dk_v[...] * gk + dv_v[...]
        a_v[h] = (grads.astype(jnp.float32) + fb_v[...] * d_normed).astype(jnp.bfloat16)

        @pl.when(h < HEADS - 1)
        def _():
            pass_on(send_a, wrap_a, h)
            choose(h + 1)

        return partial + row_sums(d_normed * wide)

    partial = lax.fori_loop(0, HEADS, backward, jnp.zeros((1, SEQ), jnp.float32))
    inner_v[...] = partial * (f * f * f * (1.0 / DW))

    @pl.when(inland)
    def _():
        for i in range(GROUP):
            send_c(i).start()

    @pl.when(first)
    def _():
        for i in range(GROUP):
            wrap_c(i, 0).start()
            wrap_c(i, 1).start()

    pass_on(send_a, wrap_a, HEADS - 1)

    def rows_at(c, base=0):
        return pl.ds(pl.multiple_of(base + c * CHUNK, CHUNK), CHUNK)

    def carry(c):
        return remote(dx_v.at[:, rows_at(c)], a_ref.at[:, rows_at(c)], dx_ss.at[c], dx_rs.at[c], section(-PLANES), t)

    def leg(c):
        return remote(dx_v.at[:, rows_at(c)], hop_v.at[:, rows_at(c)], dx_ss.at[c], hop_rs.at[c], section(-PLANES), t)

    def land(c):
        return remote(hop_v.at[:, rows_at(c)], a_ref.at[:, rows_at(c, HALF)], hop_ss.at[c], dx_rs.at[CHUNKS + c], section(1), t)

    @pl.when(porter)
    def _():
        for i in range(GROUP):
            wrap_c(i, 0).wait_recv()
        total = rc_v[0]
        for i in range(1, GROUP):
            total = total + rc_v[i]
        spread_columns(total, cb_v)
        for h in range(HEADS):
            wrap_x(h, 0).wait_recv()
            wrap_a(h, 0).wait_recv()

        def step(c, carried):
            rows = rows_at(c)
            for h in range(HEADS):
                value = ra_v[h, rows, :].astype(jnp.float32) - rx_v[h, rows, :].astype(jnp.float32) * cb_v[rows, :]
                dx_v[h, rows, :] = value.astype(jnp.bfloat16)

            @pl.when(last)
            def _():
                carry(c).start()

            @pl.when(outer)
            def _():
                leg(c).start()

            return carried

        lax.fori_loop(0, CHUNKS, step, 0)

    @pl.when(outer)
    def _():
        for c in range(CHUNKS):
            leg(c).wait_recv()
            land(c).start()
        for c in range(CHUNKS):
            leg(c).wait_send()
            land(c).wait_send()

    @pl.when(last)
    def _():
        for c in range(CHUNKS):
            carry(c).wait_send()

    @pl.when(last)
    def _():
        for c in range(2 * CHUNKS):
            rows = pl.ds(c * CHUNK, CHUNK)
            remote(a_ref.at[:, rows], a_ref.at[:, rows], dx_ss.at[0], dx_rs.at[c], section(-PLANES), t).wait_recv()

    @pl.when(first)
    def _():
        for k in range(2):
            for h in range(HEADS):
                wrap_x(h, k).wait_send()
                wrap_a(h, k).wait_send()
            for i in range(GROUP):
                wrap_c(i, k).wait_send()

    @pl.when(inland)
    def _():
        for h in range(HEADS):
            send_x(h).wait_send()
            send_a(h).wait_send()
        for i in range(GROUP):
            send_c(i).wait_send()

    for h in range(HEADS):
        stash(h).wait_send()
        pltpu.make_async_copy(lo_v.at[h], lo_ref.at[h], lo_s.at[h]).wait()
    for c in shares + [extra]:
        c.wait_send()

    @pl.when(jnp.logical_not(last))
    def _():
        for h in range(HEADS):
            send_x(h).wait_recv()
            send_a(h).wait_recv()
        for i in range(GROUP):
            send_c(i).wait_recv()


def finish(lo_ref, a_ref, x_ref, c_ref, out_ref, grad_ref, lo_v, a_v, x_v, c_v, grad_v, cb_v, in_s, out_s):
    last = lax.rem(lax.axis_index("section"), PLANES) == PLANES - 1

    def columns(ref, h):
        return ref.at[:, pl.ds(h * HDIM, HDIM)]

    scalars_in = pltpu.make_async_copy(c_ref, c_v, in_s.at[3 * HEADS])
    scalars_in.start()
    arrivals = [
        [pltpu.make_async_copy(src.at[h], dst.at[h], in_s.at[k * HEADS + h])
         for k, (src, dst) in enumerate(((lo_ref, lo_v), (a_ref, a_v), (x_ref, x_v)))]
        for h in range(HEADS)
    ]
    for copies in arrivals:
        for c in copies:
            c.start()
    scalars_in.wait()
    total = c_v[0]
    for i in range(1, GROUP):
        total = total + c_v[i]
    spread_columns(total, cb_v)
    leaving = []
    for h in range(HEADS):
        for c in arrivals[h]:
            c.wait()
        passed_on = pltpu.make_async_copy(lo_v.at[h], columns(out_ref, h), out_s.at[h])
        passed_on.start()
        leaving.append(passed_on)

        @pl.when(last)
        def _():
            grad_v[h] = a_v[h]

        @pl.when(jnp.logical_not(last))
        def _():
            value = a_v[h].astype(jnp.float32) - x_v[h].astype(jnp.float32) * cb_v[...]
            grad_v[h] = value.astype(jnp.bfloat16)

        made = pltpu.make_async_copy(grad_v.at[h], columns(grad_ref, h), out_s.at[HEADS + h])
        made.start()
        leaving.append(made)
    for c in leaving:
        c.wait()


def local(layer_input, grad_input, stashed, eviction, query_gain, key_gain):
    head_buffer = pltpu.VMEM((HEADS, SEQ, HDIM), jnp.bfloat16)
    half_buffer = pltpu.VMEM((HEADS, HALF, HDIM), jnp.bfloat16)
    column = pltpu.VMEM((SEQ, HDIM), jnp.float32)
    gain = pltpu.VMEM((1, HEADS * HDIM), jnp.float32)
    tile = pltpu.VMEM((8, LANES), jnp.float32)
    dma = pltpu.SemaphoreType.DMA
    anywhere = pl.BlockSpec(memory_space=pl.ANY)
    flat = jax.ShapeDtypeStruct((SEQ, HEADS * HDIM), jnp.bfloat16)
    split = jax.ShapeDtypeStruct((HEADS, SEQ, HDIM), jnp.bfloat16)
    lo, a, x, c = pl.pallas_call(
        kernel,
        out_shape=(split, split, split, jax.ShapeDtypeStruct((GROUP, 1, SEQ), jnp.float32)),
        in_specs=[pl.BlockSpec(memory_space=pltpu.SMEM)] + [anywhere] * 5,
        out_specs=(anywhere,) * 4,
        scratch_shapes=[gain, gain] + [head_buffer] * 8 + [column] * 3 + [half_buffer] * 4 + [
            pltpu.VMEM((GROUP, 1, HALF), jnp.float32),
            pltpu.VMEM((16, LANES), jnp.float32), pltpu.VMEM((GROUP, 16, LANES), jnp.float32),
            tile, tile, pltpu.VMEM((1, SEQ), jnp.float32), column, pltpu.VMEM((HALF, HDIM), jnp.float32),
            pltpu.SemaphoreType.REGULAR, pltpu.SemaphoreType.REGULAR,
        ] + [dma((HEADS,))] * 14 + [dma((GROUP,))] * 5 + [dma] * 2
        + [dma((2, HEADS)), dma((2, HEADS)), dma((2, GROUP)), dma((CHUNKS,)), dma((CHUNKS,)), dma((CHUNKS,)), dma((2 * CHUNKS,))],
        compiler_params=pltpu.CompilerParams(collective_id=0, has_side_effects=True, vmem_limit_bytes=60 * 2**20),
        name="tick",
    )(eviction, layer_input[0], grad_input[0], stashed[0], query_gain, key_gain)
    output, passed = pl.pallas_call(
        finish,
        out_shape=(flat, flat),
        in_specs=[anywhere] * 4,
        out_specs=(anywhere, anywhere),
        scratch_shapes=[head_buffer] * 3 + [
            pltpu.VMEM((GROUP, 1, SEQ), jnp.float32), head_buffer, column, dma((3 * HEADS + 1,)), dma((2 * HEADS,)),
        ],
        compiler_params=pltpu.CompilerParams(vmem_limit_bytes=60 * 2**20),
        name="finish",
    )(lo, a, x, c)
    return (output[None], passed[None])


def solution(mesh):
    placed = (
        P("section", None, "tensor"),
        P("section", None, "tensor"),
        P("section", None, None, "tensor"),
        P("section"),
        P("section", "tensor"),
        P("section", "tensor"),
    )
    return jax.shard_map(
        local,
        mesh=mesh,
        in_specs=placed,
        out_specs=(P("section", None, "tensor"), P("section", None, "tensor")),
        check_vma=False,
    )
```

time: 56.8 us -> 54.9 us (0.967)
  the two profiles are of different devices: /device:TPU:16 before, /device:TPU:720 now
where the time goes in v3:
time: 54.9 us; the launch traced here: 54.7 us
  Pallas kernels  53.4 us (97%)
  between operations  1.28 us (2%)
    pallas_call x1, Pallas kernels, local(): pl.pallas_call(kernel, out_shape=(split, split, split, jax.ShapeDtypeStru...  51.3 us
    pallas_call x1, Pallas kernels, local(): pl.pallas_call(finish, out_shape=(flat, flat), in_specs=[anywhere] * 4, o...  2.18 us

profile of v3, /device:TPU:720, one launch (start us, length us, event | category | flops | bytes accessed | tf_op | source)
XLA Modules:
  0.0 54.7 jit_solution(796464720405783547)
XLA Ops:
  1.3 51.3 %tick.1 = (bf16[3,512,128]{2,1,0:T(8,128)(2,1)}, bf16[3,512,128]{2,1,0:T(8,128)(2,1)}, bf16[3,512,128]{2,1,0:T(8,128)(2,1)}, f32[16,1,512]{2,1,0:T(1,128)}) custom-call(s32[1]{0:T(128)S(6)} %copy.8.ev_ref, bf16[512,384]{1,0:T(8,128)(2,1)} %bitcast.6, bf16[512,384]{1,0:T(8,128)(2,1)} %bitcast.7, bf16[2,512,384]{2,1,0:T(8,128)(2,1)} %bitcast.5, ...), custom_call_target="tpu_custom_call" | custom-call | tf_op jit(solution)/shard_map/tick/pallas_call | solution.py:469
  52.6 2.2 %finish.1 = (bf16[512,384]{1,0:T(8,128)(2,1)}, bf16[512,384]{1,0:T(8,128)(2,1)}) custom-call(bf16[3,512,128]{2,1,0:T(8,128)(2,1)} %get-tuple-element.8.lo_ref, bf16[3,512,128]{2,1,0:T(8,128)(2,1)} %get-tuple-element.9.a_ref, bf16[3,512,128]{2,1,0:T(8,128)(2,1)} %get-tuple-element.10.x_ref, f32[16,1,512]{2,1,0:T(1,128)} %get-tuple-element.11.c_ref), custom_call_target="tpu_custom_call" | custom-call | tf_op jit(solution)/shard_map/finish/pallas_call | solution.py:484

commit v4 on v3

--- a/solution.py
+++ b/solution.py
@@ -16,12 +16,14 @@
 PLANES = 12
 GROUP = 16
 HEADS = 3
+EARLY = HEADS - 1
 BLOCK = 128
 LANES = 128
 ROWS = SEQ // LANES
 CHUNK = 64
-HALF = SEQ // 2
-CHUNKS = HALF // CHUNK
+SHARES = ((0, 3), (3, 3), (6, 2))
+WIDEST = 3 * CHUNK
+CHUNKS = SEQ // CHUNK
 EPSILON = 1e-05
 SCALE = 1.0 / math.sqrt(HDIM)
 EXPONENT = SCALE * math.log2(math.e)
@@ -68,9 +70,9 @@
     ev_ref, li_ref, g_ref, st_ref, gq_ref, gk_ref,
     lo_ref, a_ref, x_ref, c_ref,
     gq_v, gk_v, li_v, g_v, own_v, away_v, got_v, x_v, a_v, lo_v, dq_v, dk_v, dv_v, dx_v, hop_v, rx_v, ra_v, rc_v,
-    part_v, parts_v, extra_v, theirs_v, inner_v, fb_v, cb_v,
+    part_v, parts_v, extra_v, theirs_v, inner_v, inners_v, c_v, fb_v, cb_v,
     ready, opened, small_s, li_s, g_s, own_s, away_s, lo_s,
-    stash_ss, stash_rs, a_ss, a_rs, x_ss, x_rs, wa_rs, wx_rs, sq_ss, sq_rs, c_ss, c_rs, wc_rs, ex_ss, ex_rs,
+    stash_ss, stash_rs, a_ss, a_rs, x_ss, x_rs, wa_rs, wx_rs, sq_ss, sq_rs, in_ss, in_rs, ex_ss, ex_rs, c_ss, c_rs, wc_rs,
     wa_ss, wx_ss, wc_ss, dx_ss, hop_ss, hop_rs, dx_rs,
 ):
     s, t = lax.axis_index("section"), lax.axis_index("tensor")
@@ -91,28 +93,24 @@
     def greet(to_s, to_t, semaphore=barrier):
         pl.semaphore_signal(semaphore, inc=1, device_id={"section": to_s, "tensor": to_t}, device_id_type=MESH)
 
-    second, porter = z == 1, z >= PLANES - 2
-    outer = z == PLANES - 2
+    second, porter = z == 1, z >= PLANES - len(SHARES)
+    outer = jnp.logical_and(porter, jnp.logical_not(last))
     greet(section(SECTIONS // 2), t)
     for by in range(1, GROUP):
         greet(s, lax.rem(t + by, GROUP))
 
-    def greet_plane(by, semaphore=barrier):
-        for to_t in range(GROUP):
-            greet(section(by), to_t, semaphore)
-
     @pl.when(jnp.logical_and(inland, jnp.logical_not(last)))
     def _():
-        greet_plane(1)
+        greet(section(1), t)
 
     @pl.when(second)
     def _():
-        greet_plane(-1)
+        greet(section(-1), t)
 
     @pl.when(first)
     def _():
-        greet_plane(PLANES - 1)
-        greet_plane(PLANES - 2)
+        for k in range(len(SHARES)):
+            greet(section(PLANES - 1 - k), t)
 
     @pl.when(porter)
     def _():
@@ -120,7 +118,8 @@
 
     @pl.when(last)
     def _():
-        greet(section(-1), t)
+        for k in range(1, len(SHARES)):
+            greet(section(-k), t)
 
     def heads_in(src, dst, sems):
         return [pltpu.make_async_copy(src.at[:, pl.ds(h * HDIM, HDIM)], dst.at[h], sems.at[h]) for h in range(HEADS)]
@@ -141,9 +140,8 @@
 
     @pl.when(porter)
     def _():
-        pl.semaphore_wait(barrier, 3 * GROUP + 1 + count(outer))
-        for to_t in range(GROUP):
-            greet(lax.rem(s - z + SECTIONS, SECTIONS), to_t, ready)
+        pl.semaphore_wait(barrier, GROUP + 3 + count(outer))
+        greet(lax.rem(s - z + SECTIONS, SECTIONS), t, ready)
 
     def squares(ref, slot):
         total = jnp.zeros((1, SEQ), jnp.float32)
@@ -166,11 +164,11 @@
 
     @pl.when(jnp.logical_not(porter))
     def _():
-        pl.semaphore_wait(barrier, GROUP + GROUP * count(z != 1))
+        pl.semaphore_wait(barrier, GROUP + count(z != 1))
 
     @pl.when(first)
     def _():
-        greet_plane(1, opened)
+        greet(section(1), t, opened)
 
     def stash(h):
         return remote(away_v.at[h], got_v.at[h], stash_ss.at[h], stash_rs.at[h], section(SECTIONS // 2), t)
@@ -223,19 +221,22 @@
         return remote(a_v.at[h], a_ref.at[h], a_ss.at[h], a_rs.at[h], section(-1), t)
 
     def wrap_x(h, k):
-        rows = pl.ds(k * HALF, HALF)
-        return remote(x_v.at[h, rows], rx_v.at[h], wx_ss.at[k, h], wx_rs.at[h], section(PLANES - 1 - k), t)
+        start, count = SHARES[k]
+        rows, held = pl.ds(start * CHUNK, count * CHUNK), pl.ds(0, count * CHUNK)
+        return remote(x_v.at[h, rows], rx_v.at[h, held], wx_ss.at[k, h], wx_rs.at[h], section(PLANES - 1 - k), t)
 
     def wrap_a(h, k):
-        rows = pl.ds(k * HALF, HALF)
-        return remote(a_v.at[h, rows], ra_v.at[h], wa_ss.at[k, h], wa_rs.at[h], section(PLANES - 1 - k), t)
-
-    def send_c(i):
-        return remote(inner_v, c_ref.at[i], c_ss.at[i], c_rs.at[i], section(-1), lax.rem(t + i, GROUP))
-
-    def wrap_c(i, k):
-        tokens = pl.ds(k * HALF, HALF)
-        return remote(inner_v.at[:, tokens], rc_v.at[i], wc_ss.at[k, i], wc_rs.at[i], section(PLANES - 1 - k), lax.rem(t + i, GROUP))
+        start, count = SHARES[k]
+        rows, held = pl.ds(start * CHUNK, count * CHUNK), pl.ds(0, count * CHUNK)
+        return remote(a_v.at[h, rows], ra_v.at[h, held], wa_ss.at[k, h], wa_rs.at[h], section(PLANES - 1 - k), t)
+
+    def share_in(i):
+        return remote(inner_v, inners_v.at[i], in_ss.at[i], in_rs.at[i], s, lax.rem(t + i, GROUP))
+
+    send_c = remote(c_v, c_ref, c_ss, c_rs, section(-1), t)
+
+    def wrap_c(k):
+        return remote(c_v, rc_v, wc_ss.at[k], wc_rs, section(PLANES - 1 - k), t)
 
     def pass_on(whole, halves, h):
         @pl.when(inland)
@@ -244,22 +245,25 @@
 
         @pl.when(first)
         def _():
-            halves(h, 0).start()
-            halves(h, 1).start()
+            for k in range(len(SHARES)):
+                halves(h, k).start()
 
     def choose(h):
         stash(h).wait_recv()
         wide = jnp.where(picked, got_v[h].astype(jnp.float32), own_v[h].astype(jnp.float32))
         x_v[h] = wide.astype(jnp.bfloat16)
-        pass_on(send_x, wrap_x, h)
+
+        @pl.when(h < EARLY)
+        def _():
+            pass_on(send_x, wrap_x, h)
 
     @pl.when(second)
     def _():
-        pl.semaphore_wait(opened, GROUP)
+        pl.semaphore_wait(opened, 1)
 
     @pl.when(first)
     def _():
-        pl.semaphore_wait(ready, 2 * GROUP)
+        pl.semaphore_wait(ready, len(SHARES))
 
     choose(0)
     extra.wait_recv()
@@ -292,10 +296,12 @@
                 dv_v[0:hi] += d_values
             dq_v[pl.ds(lo, BLOCK), :] = dot(d_scores, keys[:hi], TN) * gq
         d_normed = dq_v[...] + dk_v[...] * gk + dv_v[...]
-        a_v[h] = (grads.astype(jnp.float32) + fb_v[...] * d_normed).astype(jnp.bfloat16)
-
-        @pl.when(h < HEADS - 1)
+        a32 = grads.astype(jnp.float32) + fb_v[...] * d_normed
+        dq_v[...] = a32
+
+        @pl.when(h < EARLY)
         def _():
+            a_v[h] = a32.astype(jnp.bfloat16)
             pass_on(send_a, wrap_a, h)
             choose(h + 1)
 
@@ -303,22 +309,11 @@
 
     partial = lax.fori_loop(0, HEADS, backward, jnp.zeros((1, SEQ), jnp.float32))
     inner_v[...] = partial * (f * f * f * (1.0 / DW))
-
-    @pl.when(inland)
-    def _():
-        for i in range(GROUP):
-            send_c(i).start()
-
-    @pl.when(first)
-    def _():
-        for i in range(GROUP):
-            wrap_c(i, 0).start()
-            wrap_c(i, 1).start()
-
-    pass_on(send_a, wrap_a, HEADS - 1)
-
-    def rows_at(c, base=0):
-        return pl.ds(pl.multiple_of(base + c * CHUNK, CHUNK), CHUNK)
+    for i in range(1, GROUP):
+        share_in(i).start()
+
+    def rows_at(c):
+        return pl.ds(c * CHUNK, CHUNK)
 
     def carry(c):
         return remote(dx_v.at[:, rows_at(c)], a_ref.at[:, rows_at(c)], dx_ss.at[c], dx_rs.at[c], section(-PLANES), t)
@@ -326,92 +321,105 @@
     def leg(c):
         return remote(dx_v.at[:, rows_at(c)], hop_v.at[:, rows_at(c)], dx_ss.at[c], hop_rs.at[c], section(-PLANES), t)
 
-    def land(c):
-        return remote(hop_v.at[:, rows_at(c)], a_ref.at[:, rows_at(c, HALF)], hop_ss.at[c], dx_rs.at[CHUNKS + c], section(1), t)
+    def land(c, k):
+        at = SHARES[k][0] + c
+        return remote(hop_v.at[:, rows_at(c)], a_ref.at[:, rows_at(at)], hop_ss.at[c], dx_rs.at[at], section(k), t)
 
     @pl.when(porter)
     def _():
-        for i in range(GROUP):
-            wrap_c(i, 0).wait_recv()
-        total = rc_v[0]
-        for i in range(1, GROUP):
-            total = total + rc_v[i]
-        spread_columns(total, cb_v)
-        for h in range(HEADS):
-            wrap_x(h, 0).wait_recv()
-            wrap_a(h, 0).wait_recv()
-
-        def step(c, carried):
-            rows = rows_at(c)
-            for h in range(HEADS):
-                value = ra_v[h, rows, :].astype(jnp.float32) - rx_v[h, rows, :].astype(jnp.float32) * cb_v[rows, :]
-                dx_v[h, rows, :] = value.astype(jnp.bfloat16)
-
-            @pl.when(last)
+        wrap_c(0).wait_recv()
+        spread_columns(rc_v[...], cb_v)
+        for k, (start, chunks) in enumerate(SHARES):
+            @pl.when(z == PLANES - 1 - k)
             def _():
-                carry(c).start()
-
-            @pl.when(outer)
+                for h in range(EARLY):
+                    wrap_x(h, k).wait_recv()
+                for h in range(HEADS):
+                    wrap_a(h, k).wait_recv()
+                for c in range(chunks):
+                    rows, tokens = rows_at(c), rows_at(start + c)
+                    dx_v[EARLY, rows, :] = ra_v[EARLY, rows, :]
+                    for h in range(EARLY):
+                        value = ra_v[h, rows, :].astype(jnp.float32) - rx_v[h, rows, :].astype(jnp.float32) * cb_v[tokens, :]
+                        dx_v[h, rows, :] = value.astype(jnp.bfloat16)
+                    (leg(c) if k else carry(c)).start()
+
+    for i in range(1, GROUP):
+        share_in(i).wait_recv()
+    scalars = inner_v[...]
+    for i in range(1, GROUP):
+        scalars = scalars + inners_v[i]
+    c_v[...] = scalars
+
+    @pl.when(inland)
+    def _():
+        send_c.start()
+
+    @pl.when(first)
+    def _():
+        for k in range(len(SHARES)):
+            wrap_c(k).start()
+
+    spread_columns(scalars, cb_v)
+    a_v[EARLY] = (dq_v[...] - x_v[EARLY].astype(jnp.float32) * cb_v[...]).astype(jnp.bfloat16)
+    pass_on(send_a, wrap_a, EARLY)
+
+    @pl.when(outer)
+    def _():
+        for k in range(1, len(SHARES)):
+            @pl.when(z == PLANES - 1 - k)
             def _():
-                leg(c).start()
-
-            return carried
-
-        lax.fori_loop(0, CHUNKS, step, 0)
-
-    @pl.when(outer)
+                for c in range(SHARES[k][1]):
+                    leg(c).wait_recv()
+                    land(c, k).start()
+                for c in range(SHARES[k][1]):
+                    leg(c).wait_send()
+                    land(c, k).wait_send()
+
+    @pl.when(last)
+    def _():
+        for c in range(SHARES[0][1]):
+            carry(c).wait_send()
+
+    @pl.when(last)
     def _():
         for c in range(CHUNKS):
-            leg(c).wait_recv()
-            land(c).start()
-        for c in range(CHUNKS):
-            leg(c).wait_send()
-            land(c).wait_send()
-
-    @pl.when(last)
-    def _():
-        for c in range(CHUNKS):
-            carry(c).wait_send()
-
-    @pl.when(last)
-    def _():
-        for c in range(2 * CHUNKS):
             rows = pl.ds(c * CHUNK, CHUNK)
             remote(a_ref.at[:, rows], a_ref.at[:, rows], dx_ss.at[0], dx_rs.at[c], section(-PLANES), t).wait_recv()
 
     @pl.when(first)
     def _():
-        for k in range(2):
+        for k in range(len(SHARES)):
+            for h in range(EARLY):
+                wrap_x(h, k).wait_send()
             for h in range(HEADS):
-                wrap_x(h, k).wait_send()
                 wrap_a(h, k).wait_send()
-            for i in range(GROUP):
-                wrap_c(i, k).wait_send()
+            wrap_c(k).wait_send()
 
     @pl.when(inland)
     def _():
+        for h in range(EARLY):
+            send_x(h).wait_send()
         for h in range(HEADS):
-            send_x(h).wait_send()
             send_a(h).wait_send()
-        for i in range(GROUP):
-            send_c(i).wait_send()
+        send_c.wait_send()
 
     for h in range(HEADS):
         stash(h).wait_send()
         pltpu.make_async_copy(lo_v.at[h], lo_ref.at[h], lo_s.at[h]).wait()
-    for c in shares + [extra]:
+    for c in shares + [share_in(i) for i in range(1, GROUP)] + [extra]:
         c.wait_send()
 
     @pl.when(jnp.logical_not(last))
     def _():
+        for h in range(EARLY):
+            send_x(h).wait_recv()
         for h in range(HEADS):
-            send_x(h).wait_recv()
             send_a(h).wait_recv()
-        for i in range(GROUP):
-            send_c(i).wait_recv()
-
-
-def finish(lo_ref, a_ref, x_ref, c_ref, out_ref, grad_ref, lo_v, a_v, x_v, c_v, grad_v, cb_v, in_s, out_s):
+        send_c.wait_recv()
+
+
+def finish(lo_ref, a_ref, x_ref, c_ref, out_ref, grad_ref, lo_v, a_v, x_v, c_v, cb_v, in_s, out_s):
     last = lax.rem(lax.axis_index("section"), PLANES) == PLANES - 1
 
     def columns(ref, h):
@@ -421,17 +429,14 @@
     scalars_in.start()
     arrivals = [
         [pltpu.make_async_copy(src.at[h], dst.at[h], in_s.at[k * HEADS + h])
-         for k, (src, dst) in enumerate(((lo_ref, lo_v), (a_ref, a_v), (x_ref, x_v)))]
+         for k, (src, dst) in enumerate(((lo_ref, lo_v), (a_ref, a_v), (x_ref, x_v))) if k < 2 or h < EARLY]
         for h in range(HEADS)
     ]
     for copies in arrivals:
         for c in copies:
             c.start()
     scalars_in.wait()
-    total = c_v[0]
-    for i in range(1, GROUP):
-        total = total + c_v[i]
-    spread_columns(total, cb_v)
+    spread_columns(c_v[...], cb_v)
     leaving = []
     for h in range(HEADS):
         for c in arrivals[h]:
@@ -440,16 +445,13 @@
         passed_on.start()
         leaving.append(passed_on)
 
-        @pl.when(last)
-        def _():
-            grad_v[h] = a_v[h]
-
-        @pl.when(jnp.logical_not(last))
-        def _():
-            value = a_v[h].astype(jnp.float32) - x_v[h].astype(jnp.float32) * cb_v[...]
-            grad_v[h] = value.astype(jnp.bfloat16)
-
-        made = pltpu.make_async_copy(grad_v.at[h], columns(grad_ref, h), out_s.at[HEADS + h])
+        if h < EARLY:
+            @pl.when(jnp.logical_not(last))
+            def _():
+                value = a_v[h].astype(jnp.float32) - x_v[h].astype(jnp.float32) * cb_v[...]
+                a_v[h] = value.astype(jnp.bfloat16)
+
+        made = pltpu.make_async_copy(a_v.at[h], columns(grad_ref, h), out_s.at[HEADS + h])
         made.start()
         leaving.append(made)
     for c in leaving:
@@ -458,26 +460,27 @@
 
 def local(layer_input, grad_input, stashed, eviction, query_gain, key_gain):
     head_buffer = pltpu.VMEM((HEADS, SEQ, HDIM), jnp.bfloat16)
-    half_buffer = pltpu.VMEM((HEADS, HALF, HDIM), jnp.bfloat16)
+    share_buffer = pltpu.VMEM((HEADS, WIDEST, HDIM), jnp.bfloat16)
     column = pltpu.VMEM((SEQ, HDIM), jnp.float32)
     gain = pltpu.VMEM((1, HEADS * HDIM), jnp.float32)
     tile = pltpu.VMEM((8, LANES), jnp.float32)
+    row = pltpu.VMEM((1, SEQ), jnp.float32)
     dma = pltpu.SemaphoreType.DMA
     anywhere = pl.BlockSpec(memory_space=pl.ANY)
     flat = jax.ShapeDtypeStruct((SEQ, HEADS * HDIM), jnp.bfloat16)
     split = jax.ShapeDtypeStruct((HEADS, SEQ, HDIM), jnp.bfloat16)
     lo, a, x, c = pl.pallas_call(
         kernel,
-        out_shape=(split, split, split, jax.ShapeDtypeStruct((GROUP, 1, SEQ), jnp.float32)),
+        out_shape=(split, split, split, jax.ShapeDtypeStruct((1, SEQ), jnp.float32)),
         in_specs=[pl.BlockSpec(memory_space=pltpu.SMEM)] + [anywhere] * 5,
         out_specs=(anywhere,) * 4,
-        scratch_shapes=[gain, gain] + [head_buffer] * 8 + [column] * 3 + [half_buffer] * 4 + [
-            pltpu.VMEM((GROUP, 1, HALF), jnp.float32),
+        scratch_shapes=[gain, gain] + [head_buffer] * 8 + [column] * 3 + [share_buffer] * 4 + [
+            row,
             pltpu.VMEM((16, LANES), jnp.float32), pltpu.VMEM((GROUP, 16, LANES), jnp.float32),
-            tile, tile, pltpu.VMEM((1, SEQ), jnp.float32), column, pltpu.VMEM((HALF, HDIM), jnp.float32),
+            tile, tile, row, pltpu.VMEM((GROUP, 1, SEQ), jnp.float32), row, column, column,
             pltpu.SemaphoreType.REGULAR, pltpu.SemaphoreType.REGULAR,
-        ] + [dma((HEADS,))] * 14 + [dma((GROUP,))] * 5 + [dma] * 2
-        + [dma((2, HEADS)), dma((2, HEADS)), dma((2, GROUP)), dma((CHUNKS,)), dma((CHUNKS,)), dma((CHUNKS,)), dma((2 * CHUNKS,))],
+        ] + [dma((HEADS,))] * 14 + [dma((GROUP,))] * 4 + [dma] * 5
+        + [dma((len(SHARES), HEADS))] * 2 + [dma((len(SHARES),))] + [dma((CHUNKS,))] * 4,
         compiler_params=pltpu.CompilerParams(collective_id=0, has_side_effects=True, vmem_limit_bytes=60 * 2**20),
         name="tick",
     )(eviction, layer_input[0], grad_input[0], stashed[0], query_gain, key_gain)
@@ -486,9 +489,7 @@
         out_shape=(flat, flat),
         in_specs=[anywhere] * 4,
         out_specs=(anywhere, anywhere),
-        scratch_shapes=[head_buffer] * 3 + [
-            pltpu.VMEM((GROUP, 1, SEQ), jnp.float32), head_buffer, column, dma((3 * HEADS + 1,)), dma((2 * HEADS,)),
-        ],
+        scratch_shapes=[head_buffer] * 3 + [row, column, dma((3 * HEADS + 1,)), dma((2 * HEADS,))],
         compiler_params=pltpu.CompilerParams(vmem_limit_bytes=60 * 2**20),
         name="finish",
     )(lo, a, x, c)

time: 54.9 us -> 50.4 us (0.918)
  Pallas kernels: 53.4 us -> 48.9 us
    pallas_call x1, Pallas kernels: 51.3 us -> 46.7 us  [local(): pl.pallas_call(kernel, out_shape=(split, split, split, jax.ShapeDtypeStru...]
where the time goes in v4:
time: 50.4 us; the launch traced here: 50.2 us
  Pallas kernels  48.9 us (97%)
  between operations  1.28 us (3%)
    pallas_call x1, Pallas kernels, local(): pl.pallas_call(kernel, out_shape=(split, split, split, jax.ShapeDtypeStru...  46.7 us
    pallas_call x1, Pallas kernels, local(): pl.pallas_call(finish, out_shape=(flat, flat), in_specs=[anywhere] * 4, o...  2.13 us

profile of v4, /device:TPU:720, one launch (start us, length us, event | category | flops | bytes accessed | tf_op | source)
XLA Modules:
  0.0 50.2 jit_solution(13683791430863033376)
XLA Ops:
  1.3 46.7 %tick.1 = (bf16[3,512,128]{2,1,0:T(8,128)(2,1)}, bf16[3,512,128]{2,1,0:T(8,128)(2,1)}, bf16[3,512,128]{2,1,0:T(8,128)(2,1)}, f32[1,512]{1,0:T(1,128)}) custom-call(s32[1]{0:T(128)S(6)} %copy.8.ev_ref, bf16[512,384]{1,0:T(8,128)(2,1)} %bitcast.6, bf16[512,384]{1,0:T(8,128)(2,1)} %bitcast.7, bf16[2,512,384]{2,1,0:T(8,128)(2,1)} %bitcast.5, f32[1,384]{1,0:T(1,128)} %gq_ref.1, ...), custom_call_target="tpu_custom_call" | custom-call | tf_op jit(solution)/shard_map/tick/pallas_call | solution.py:472
  48.0 2.1 %finish.1 = (bf16[512,384]{1,0:T(8,128)(2,1)}, bf16[512,384]{1,0:T(8,128)(2,1)}) custom-call(bf16[3,512,128]{2,1,0:T(8,128)(2,1)} %get-tuple-element.8.lo_ref, bf16[3,512,128]{2,1,0:T(8,128)(2,1)} %get-tuple-element.9.a_ref, bf16[3,512,128]{2,1,0:T(8,128)(2,1)} %get-tuple-element.10.x_ref, f32[1,512]{1,0:T(1,128)} %get-tuple-element.11.c_ref), custom_call_target="tpu_custom_call" | custom-call | tf_op jit(solution)/shard_map/finish/pallas_call | solution.py:487

commit v5 on v4

--- a/solution.py
+++ b/solution.py
@@ -19,7 +19,7 @@
 EARLY = HEADS - 1
 BLOCK = 128
 LANES = 128
-ROWS = SEQ // LANES
+
 CHUNK = 64
 SHARES = ((0, 3), (3, 3), (6, 2))
 WIDEST = 3 * CHUNK
@@ -47,10 +47,6 @@
     for lo in range(0, row.shape[1], LANES):
         block = jnp.broadcast_to(row[:, lo : lo + LANES], (LANES, LANES))
         out_ref[pl.ds(lo, LANES), :] = block.T
-
-
-def one_row(rows):
-    return jnp.concatenate([rows[b : b + 1] for b in range(ROWS)], axis=1)
 
 
 def block_weights(keys, queries, lo, hi):
@@ -71,9 +67,9 @@
     lo_ref, a_ref, x_ref, c_ref,
     gq_v, gk_v, li_v, g_v, own_v, away_v, got_v, x_v, a_v, lo_v, dq_v, dk_v, dv_v, dx_v, hop_v, rx_v, ra_v, rc_v,
     part_v, parts_v, extra_v, theirs_v, inner_v, inners_v, c_v, fb_v, cb_v,
-    ready, opened, small_s, li_s, g_s, own_s, away_s, lo_s,
-    stash_ss, stash_rs, a_ss, a_rs, x_ss, x_rs, wa_rs, wx_rs, sq_ss, sq_rs, in_ss, in_rs, ex_ss, ex_rs, c_ss, c_rs, wc_rs,
-    wa_ss, wx_ss, wc_ss, dx_ss, hop_ss, hop_rs, dx_rs,
+    ready, opened, small_s, li_s, g_s, own_s, away_s, lo_s, stash_ss, stash_rs,
+    a_ss, a_rs, x_ss, x_rs, wa_ss, wa_rs, wx_ss, wx_rs, sq_ss, sq_rs, in_ss, in_rs, ex_ss, ex_rs,
+    c_ss, c_rs, wc_ss, wc_rs, dx_ss, dx_rs, hop_ss, hop_rs,
 ):
     s, t = lax.axis_index("section"), lax.axis_index("tensor")
     z = lax.rem(s, PLANES)
@@ -88,6 +84,15 @@
             src_ref=src, dst_ref=dst, send_sem=ss, recv_sem=rs,
             device_id={"section": to_s, "tensor": to_t}, device_id_type=MESH)
 
+    def settle(ref, semaphore):
+        pltpu.make_async_copy(ref, ref, semaphore).wait()
+
+    def arrived(ref, semaphore):
+        remote(ref, ref, semaphore, semaphore, section(1), t).wait_recv()
+
+    def sent(ref, semaphore):
+        remote(ref, ref, semaphore, semaphore, section(1), t).wait_send()
+
     barrier = pltpu.get_barrier_semaphore()
 
     def greet(to_s, to_t, semaphore=barrier):
@@ -122,15 +127,15 @@
             greet(section(-k), t)
 
     def heads_in(src, dst, sems):
-        return [pltpu.make_async_copy(src.at[:, pl.ds(h * HDIM, HDIM)], dst.at[h], sems.at[h]) for h in range(HEADS)]
+        return [pltpu.make_async_copy(src.at[:, pl.ds(h * HDIM, HDIM)], dst.at[h], sems) for h in range(HEADS)]
 
     away_in = heads_in(st_ref.at[1], away_v, away_s)
     li_in = heads_in(li_ref, li_v, li_s)
     own_in = heads_in(st_ref.at[0], own_v, own_s)
     g_in = heads_in(g_ref, g_v, g_s)
     small_in = [
-        pltpu.make_async_copy(gq_ref, gq_v, small_s.at[1]),
-        pltpu.make_async_copy(gk_ref, gk_v, small_s.at[2]),
+        pltpu.make_async_copy(gq_ref, gq_v, small_s.at[0]),
+        pltpu.make_async_copy(gk_ref, gk_v, small_s.at[1]),
     ]
     for c in away_in + li_in + own_in + small_in + g_in:
         c.start()
@@ -148,19 +153,14 @@
         for h in range(HEADS):
             wide = ref[h].astype(jnp.float32)
             total = total + row_sums(wide * wide)
-        for b in range(ROWS):
-            part_v[pl.ds(slot * ROWS + b, 1), :] = total[:, b * LANES : (b + 1) * LANES]
-
-    for c in away_in:
-        c.wait()
+        part_v[:, slot * SEQ : (slot + 1) * SEQ] = total
+
+    settle(away_v, away_s)
     squares(away_v, 2)
-    for c in li_in:
-        c.wait()
+    settle(li_v, li_s)
     squares(li_v, 0)
-    for c in own_in:
-        c.wait()
+    settle(own_v, own_s)
     squares(own_v, 1)
-    part_v[12:16] = jnp.zeros((4, LANES), jnp.float32)
 
     @pl.when(jnp.logical_not(porter))
     def _():
@@ -171,20 +171,21 @@
         greet(section(1), t, opened)
 
     def stash(h):
-        return remote(away_v.at[h], got_v.at[h], stash_ss.at[h], stash_rs.at[h], section(SECTIONS // 2), t)
-
-    shares = [remote(part_v, parts_v.at[i], sq_ss.at[i], sq_rs.at[i], s, lax.rem(t + i, GROUP)) for i in range(1, GROUP)]
+        return remote(away_v.at[h], got_v.at[h], stash_ss, stash_rs.at[h], section(SECTIONS // 2), t)
+
+    shares = [remote(part_v, parts_v.at[i], sq_ss, sq_rs, s, lax.rem(t + i, GROUP)) for i in range(1, GROUP)]
     for c in shares:
         c.start()
     stash(0).start()
-    for c in small_in + g_in:
+    for c in small_in:
         c.wait()
-    for c in shares:
-        c.wait_recv()
+    settle(g_v, g_s)
+    others = pl.ds(1, GROUP - 1)
+    arrived(parts_v.at[others], sq_rs)
     totals = part_v[...]
     for i in range(1, GROUP):
         totals = totals + parts_v[i]
-    extra_v[...] = totals[8:16]
+    extra_v[...] = totals[:, 2 * SEQ :]
     extra = remote(extra_v, theirs_v, ex_ss, ex_rs, section(SECTIONS // 2), t)
     extra.start()
     stash(1).start()
@@ -193,7 +194,7 @@
     def factor_of(total):
         return lax.rsqrt(total / DW + EPSILON)
 
-    spread_columns(factor_of(one_row(totals[0:ROWS])), fb_v)
+    spread_columns(factor_of(totals[:, :SEQ]), fb_v)
 
     def forward(h, carry):
         cols = pl.ds(pl.multiple_of(h * HDIM, HDIM), HDIM)
@@ -207,7 +208,7 @@
             weights = block_weights(keys, queries, lo, hi).astype(jnp.bfloat16)
             mixed = dot(weights, values[:hi], TN)
             lo_v[h, pl.ds(lo, BLOCK), :] = (wide[lo:hi] + mixed).astype(jnp.bfloat16)
-        pltpu.make_async_copy(lo_v.at[h], lo_ref.at[h], lo_s.at[h]).start()
+        pltpu.make_async_copy(lo_v.at[h], lo_ref.at[h], lo_s).start()
         return carry
 
     lax.fori_loop(0, HEADS, forward, 0)
@@ -215,28 +216,28 @@
     picked = jnp.full((SEQ, HDIM), ev_ref[0], jnp.int32) == 1
 
     def send_x(h):
-        return remote(x_v.at[h], x_ref.at[h], x_ss.at[h], x_rs.at[h], section(-1), t)
+        return remote(x_v.at[h], x_ref.at[h], x_ss, x_rs, section(-1), t)
 
     def send_a(h):
-        return remote(a_v.at[h], a_ref.at[h], a_ss.at[h], a_rs.at[h], section(-1), t)
+        return remote(a_v.at[h], a_ref.at[h], a_ss, a_rs, section(-1), t)
 
     def wrap_x(h, k):
         start, count = SHARES[k]
         rows, held = pl.ds(start * CHUNK, count * CHUNK), pl.ds(0, count * CHUNK)
-        return remote(x_v.at[h, rows], rx_v.at[h, held], wx_ss.at[k, h], wx_rs.at[h], section(PLANES - 1 - k), t)
+        return remote(x_v.at[h, rows], rx_v.at[h, held], wx_ss, wx_rs, section(PLANES - 1 - k), t)
 
     def wrap_a(h, k):
         start, count = SHARES[k]
         rows, held = pl.ds(start * CHUNK, count * CHUNK), pl.ds(0, count * CHUNK)
-        return remote(a_v.at[h, rows], ra_v.at[h, held], wa_ss.at[k, h], wa_rs.at[h], section(PLANES - 1 - k), t)
+        return remote(a_v.at[h, rows], ra_v.at[h, held], wa_ss, wa_rs, section(PLANES - 1 - k), t)
 
     def share_in(i):
-        return remote(inner_v, inners_v.at[i], in_ss.at[i], in_rs.at[i], s, lax.rem(t + i, GROUP))
+        return remote(inner_v, inners_v.at[i], in_ss, in_rs, s, lax.rem(t + i, GROUP))
 
     send_c = remote(c_v, c_ref, c_ss, c_rs, section(-1), t)
 
     def wrap_c(k):
-        return remote(c_v, rc_v, wc_ss.at[k], wc_rs, section(PLANES - 1 - k), t)
+        return remote(c_v, rc_v, wc_ss, wc_rs, section(PLANES - 1 - k), t)
 
     def pass_on(whole, halves, h):
         @pl.when(inland)
@@ -268,7 +269,7 @@
     choose(0)
     extra.wait_recv()
     evicted = jnp.full((1, SEQ), ev_ref[0], jnp.int32) == 1
-    f = factor_of(jnp.where(evicted, one_row(theirs_v[0:ROWS]), one_row(totals[4:8])))
+    f = factor_of(jnp.where(evicted, theirs_v[...], totals[:, SEQ : 2 * SEQ]))
     spread_columns(f, fb_v)
 
     def backward(h, partial):
@@ -316,14 +317,14 @@
         return pl.ds(c * CHUNK, CHUNK)
 
     def carry(c):
-        return remote(dx_v.at[:, rows_at(c)], a_ref.at[:, rows_at(c)], dx_ss.at[c], dx_rs.at[c], section(-PLANES), t)
+        return remote(dx_v.at[:, rows_at(c)], a_ref.at[:, rows_at(c)], dx_ss, dx_rs, section(-PLANES), t)
 
     def leg(c):
-        return remote(dx_v.at[:, rows_at(c)], hop_v.at[:, rows_at(c)], dx_ss.at[c], hop_rs.at[c], section(-PLANES), t)
+        return remote(dx_v.at[:, rows_at(c)], hop_v.at[:, rows_at(c)], dx_ss, hop_rs.at[c], section(-PLANES), t)
 
     def land(c, k):
         at = SHARES[k][0] + c
-        return remote(hop_v.at[:, rows_at(c)], a_ref.at[:, rows_at(at)], hop_ss.at[c], dx_rs.at[at], section(k), t)
+        return remote(hop_v.at[:, rows_at(c)], a_ref.at[:, rows_at(at)], hop_ss, dx_rs, section(k), t)
 
     @pl.when(porter)
     def _():
@@ -332,10 +333,8 @@
         for k, (start, chunks) in enumerate(SHARES):
             @pl.when(z == PLANES - 1 - k)
             def _():
-                for h in range(EARLY):
-                    wrap_x(h, k).wait_recv()
-                for h in range(HEADS):
-                    wrap_a(h, k).wait_recv()
+                arrived(rx_v.at[pl.ds(0, EARLY), pl.ds(0, chunks * CHUNK)], wx_rs)
+                arrived(ra_v.at[:, pl.ds(0, chunks * CHUNK)], wa_rs)
                 for c in range(chunks):
                     rows, tokens = rows_at(c), rows_at(start + c)
                     dx_v[EARLY, rows, :] = ra_v[EARLY, rows, :]
@@ -344,8 +343,7 @@
                         dx_v[h, rows, :] = value.astype(jnp.bfloat16)
                     (leg(c) if k else carry(c)).start()
 
-    for i in range(1, GROUP):
-        share_in(i).wait_recv()
+    arrived(inners_v.at[others], in_rs)
     scalars = inner_v[...]
     for i in range(1, GROUP):
         scalars = scalars + inners_v[i]
@@ -372,50 +370,40 @@
                 for c in range(SHARES[k][1]):
                     leg(c).wait_recv()
                     land(c, k).start()
-                for c in range(SHARES[k][1]):
-                    leg(c).wait_send()
-                    land(c, k).wait_send()
+                rows = pl.ds(0, SHARES[k][1] * CHUNK)
+                sent(dx_v.at[:, rows], dx_ss)
+                sent(hop_v.at[:, rows], hop_ss)
 
     @pl.when(last)
     def _():
-        for c in range(SHARES[0][1]):
-            carry(c).wait_send()
+        sent(dx_v.at[:, pl.ds(0, SHARES[0][1] * CHUNK)], dx_ss)
 
     @pl.when(last)
     def _():
-        for c in range(CHUNKS):
-            rows = pl.ds(c * CHUNK, CHUNK)
-            remote(a_ref.at[:, rows], a_ref.at[:, rows], dx_ss.at[0], dx_rs.at[c], section(-PLANES), t).wait_recv()
+        arrived(a_ref, dx_rs)
 
     @pl.when(first)
     def _():
-        for k in range(len(SHARES)):
-            for h in range(EARLY):
-                wrap_x(h, k).wait_send()
-            for h in range(HEADS):
-                wrap_a(h, k).wait_send()
-            wrap_c(k).wait_send()
+        sent(x_ref, wx_ss)
+        sent(a_v, wa_ss)
+        sent(inners_v.at[pl.ds(0, len(SHARES))], wc_ss)
 
     @pl.when(inland)
     def _():
-        for h in range(EARLY):
-            send_x(h).wait_send()
-        for h in range(HEADS):
-            send_a(h).wait_send()
+        sent(x_ref, x_ss)
+        sent(a_v, a_ss)
         send_c.wait_send()
 
-    for h in range(HEADS):
-        stash(h).wait_send()
-        pltpu.make_async_copy(lo_v.at[h], lo_ref.at[h], lo_s.at[h]).wait()
-    for c in shares + [share_in(i) for i in range(1, GROUP)] + [extra]:
-        c.wait_send()
+    sent(away_v, stash_ss)
+    settle(lo_v, lo_s)
+    sent(parts_v.at[others], sq_ss)
+    sent(inners_v.at[others], in_ss)
+    extra.wait_send()
 
     @pl.when(jnp.logical_not(last))
     def _():
-        for h in range(EARLY):
-            send_x(h).wait_recv()
-        for h in range(HEADS):
-            send_a(h).wait_recv()
+        arrived(x_ref, x_rs)
+        arrived(a_ref, a_rs)
         send_c.wait_recv()
 
 
@@ -463,24 +451,23 @@
     share_buffer = pltpu.VMEM((HEADS, WIDEST, HDIM), jnp.bfloat16)
     column = pltpu.VMEM((SEQ, HDIM), jnp.float32)
     gain = pltpu.VMEM((1, HEADS * HDIM), jnp.float32)
-    tile = pltpu.VMEM((8, LANES), jnp.float32)
     row = pltpu.VMEM((1, SEQ), jnp.float32)
     dma = pltpu.SemaphoreType.DMA
     anywhere = pl.BlockSpec(memory_space=pl.ANY)
     flat = jax.ShapeDtypeStruct((SEQ, HEADS * HDIM), jnp.bfloat16)
     split = jax.ShapeDtypeStruct((HEADS, SEQ, HDIM), jnp.bfloat16)
+    early = jax.ShapeDtypeStruct((EARLY, SEQ, HDIM), jnp.bfloat16)
     lo, a, x, c = pl.pallas_call(
         kernel,
-        out_shape=(split, split, split, jax.ShapeDtypeStruct((1, SEQ), jnp.float32)),
+        out_shape=(split, split, early, jax.ShapeDtypeStruct((1, SEQ), jnp.float32)),
         in_specs=[pl.BlockSpec(memory_space=pltpu.SMEM)] + [anywhere] * 5,
         out_specs=(anywhere,) * 4,
         scratch_shapes=[gain, gain] + [head_buffer] * 8 + [column] * 3 + [share_buffer] * 4 + [
             row,
-            pltpu.VMEM((16, LANES), jnp.float32), pltpu.VMEM((GROUP, 16, LANES), jnp.float32),
-            tile, tile, row, pltpu.VMEM((GROUP, 1, SEQ), jnp.float32), row, column, column,
+            pltpu.VMEM((1, 3 * SEQ), jnp.float32), pltpu.VMEM((GROUP, 1, 3 * SEQ), jnp.float32),
+            row, row, row, pltpu.VMEM((GROUP, 1, SEQ), jnp.float32), row, column, column,
             pltpu.SemaphoreType.REGULAR, pltpu.SemaphoreType.REGULAR,
-        ] + [dma((HEADS,))] * 14 + [dma((GROUP,))] * 4 + [dma] * 5
-        + [dma((len(SHARES), HEADS))] * 2 + [dma((len(SHARES),))] + [dma((CHUNKS,))] * 4,
+        ] + [dma((2,))] + [dma] * 6 + [dma((HEADS,))] + [dma] * 21 + [dma((SHARES[0][1],))],
         compiler_params=pltpu.CompilerParams(collective_id=0, has_side_effects=True, vmem_limit_bytes=60 * 2**20),
         name="tick",
     )(eviction, layer_input[0], grad_input[0], stashed[0], query_gain, key_gain)

time: 50.4 us -> 47.4 us (0.940)
  the two profiles are of different devices: /device:TPU:720 before, /device:TPU:640 now
where the time goes in v5:
time: 47.4 us; the launch traced here: 47.2 us
  Pallas kernels  46 us (97%)
  between operations  1.28 us (3%)
    pallas_call x1, Pallas kernels, local(): pl.pallas_call(kernel, out_shape=(split, split, early, jax.ShapeDtypeStru...  43.8 us
    pallas_call x1, Pallas kernels, local(): pl.pallas_call(finish, out_shape=(flat, flat), in_specs=[anywhere] * 4, o...  2.13 us

profile of v5, /device:TPU:640, one launch (start us, length us, event | category | flops | bytes accessed | tf_op | source)
XLA Modules:
  0.0 47.2 jit_solution(12522605018360213711)
XLA Ops:
  1.3 43.8 %tick.1 = (bf16[3,512,128]{2,1,0:T(8,128)(2,1)}, bf16[3,512,128]{2,1,0:T(8,128)(2,1)}, bf16[2,512,128]{2,1,0:T(8,128)(2,1)}, f32[1,512]{1,0:T(1,128)}) custom-call(s32[1]{0:T(128)S(6)} %copy.8.ev_ref, bf16[512,384]{1,0:T(8,128)(2,1)} %bitcast.6, bf16[512,384]{1,0:T(8,128)(2,1)} %bitcast.7, bf16[2,512,384]{2,1,0:T(8,128)(2,1)} %bitcast.5, f32[1,384]{1,0:T(1,128)} %gq_ref.1, ...), custom_call_target="tpu_custom_call" | custom-call | tf_op jit(solution)/shard_map/tick/pallas_call | solution.py:460
  45.1 2.1 %finish.1 = (bf16[512,384]{1,0:T(8,128)(2,1)}, bf16[512,384]{1,0:T(8,128)(2,1)}) custom-call(bf16[3,512,128]{2,1,0:T(8,128)(2,1)} %get-tuple-element.8.lo_ref, bf16[3,512,128]{2,1,0:T(8,128)(2,1)} %get-tuple-element.9.a_ref, bf16[2,512,128]{2,1,0:T(8,128)(2,1)} %get-tuple-element.10.x_ref, f32[1,512]{1,0:T(1,128)} %get-tuple-element.11.c_ref), custom_call_target="tpu_custom_call" | custom-call | tf_op jit(solution)/shard_map/finish/pallas_call | solution.py:474

commit v6 on v5

--- a/solution.py
+++ b/solution.py
@@ -21,8 +21,9 @@
 LANES = 128
 
 CHUNK = 64
-SHARES = ((0, 3), (3, 3), (6, 2))
-WIDEST = 3 * CHUNK
+SHARES = ((0, 4), (4, 2), (6, 2))
+WIDEST = 4 * CHUNK
+HALF = SEQ // 2
 CHUNKS = SEQ // CHUNK
 EPSILON = 1e-05
 SCALE = 1.0 / math.sqrt(HDIM)
@@ -69,7 +70,7 @@
     part_v, parts_v, extra_v, theirs_v, inner_v, inners_v, c_v, fb_v, cb_v,
     ready, opened, small_s, li_s, g_s, own_s, away_s, lo_s, stash_ss, stash_rs,
     a_ss, a_rs, x_ss, x_rs, wa_ss, wa_rs, wx_ss, wx_rs, sq_ss, sq_rs, in_ss, in_rs, ex_ss, ex_rs,
-    c_ss, c_rs, wc_ss, wc_rs, dx_ss, dx_rs, hop_ss, hop_rs,
+    c_ss, c_rs, wc_ss, wc_rs, wl_ss, dx_ss, dx_rs, hop_ss, hop_rs,
 ):
     s, t = lax.axis_index("section"), lax.axis_index("tensor")
     z = lax.rem(s, PLANES)
@@ -215,16 +216,19 @@
 
     picked = jnp.full((SEQ, HDIM), ev_ref[0], jnp.int32) == 1
 
-    def send_x(h):
-        return remote(x_v.at[h], x_ref.at[h], x_ss, x_rs, section(-1), t)
-
-    def send_a(h):
-        return remote(a_v.at[h], a_ref.at[h], a_ss, a_rs, section(-1), t)
-
-    def wrap_x(h, k):
+    upper, lower = pl.ds(0, HALF), pl.ds(HALF, HALF)
+
+    def send_x(h, k):
+        rows = (upper, lower)[k]
+        return remote(x_v.at[h, rows], x_ref.at[2 * h + k], x_ss, x_rs, section(-1), t)
+
+    def send_a(h, rows):
+        return remote(a_v.at[h, rows], a_ref.at[h, rows], a_ss, a_rs, section(-1), t)
+
+    def wrap_x(h, k, semaphore=wx_ss):
         start, count = SHARES[k]
         rows, held = pl.ds(start * CHUNK, count * CHUNK), pl.ds(0, count * CHUNK)
-        return remote(x_v.at[h, rows], rx_v.at[h, held], wx_ss, wx_rs, section(PLANES - 1 - k), t)
+        return remote(x_v.at[h, rows], rx_v.at[h, held], semaphore, wx_rs, section(PLANES - 1 - k), t)
 
     def wrap_a(h, k):
         start, count = SHARES[k]
@@ -239,24 +243,32 @@
     def wrap_c(k):
         return remote(c_v, rc_v, wc_ss, wc_rs, section(PLANES - 1 - k), t)
 
-    def pass_on(whole, halves, h):
-        @pl.when(inland)
-        def _():
-            whole(h).start()
-
+    def to_porters(piece, h):
         @pl.when(first)
         def _():
             for k in range(len(SHARES)):
-                halves(h, k).start()
+                piece(h, k).start()
 
     def choose(h):
         stash(h).wait_recv()
         wide = jnp.where(picked, got_v[h].astype(jnp.float32), own_v[h].astype(jnp.float32))
         x_v[h] = wide.astype(jnp.bfloat16)
 
+        @pl.when(inland)
+        def _():
+            send_x(h, 0).start()
+
         @pl.when(h < EARLY)
         def _():
-            pass_on(send_x, wrap_x, h)
+            to_porters(wrap_x, h)
+
+            @pl.when(inland)
+            def _():
+                send_x(h, 1).start()
+
+        @pl.when(jnp.logical_and(first, h == EARLY))
+        def _():
+            wrap_x(EARLY, 0, wl_ss).start()
 
     @pl.when(second)
     def _():
@@ -299,11 +311,26 @@
         d_normed = dq_v[...] + dk_v[...] * gk + dv_v[...]
         a32 = grads.astype(jnp.float32) + fb_v[...] * d_normed
         dq_v[...] = a32
+        a_v[h] = a32.astype(jnp.bfloat16)
+
+        @pl.when(inland)
+        def _():
+            send_a(h, upper).start()
 
         @pl.when(h < EARLY)
         def _():
-            a_v[h] = a32.astype(jnp.bfloat16)
-            pass_on(send_a, wrap_a, h)
+            to_porters(wrap_a, h)
+
+            @pl.when(inland)
+            def _():
+                send_a(h, lower).start()
+
+        @pl.when(jnp.logical_and(first, h == EARLY))
+        def _():
+            wrap_a(EARLY, 0).start()
+
+        @pl.when(h < EARLY)
+        def _():
             choose(h + 1)
 
         return partial + row_sums(d_normed * wide)
@@ -333,12 +360,14 @@
         for k, (start, chunks) in enumerate(SHARES):
             @pl.when(z == PLANES - 1 - k)
             def _():
-                arrived(rx_v.at[pl.ds(0, EARLY), pl.ds(0, chunks * CHUNK)], wx_rs)
+                paired = EARLY if k else HEADS
+                arrived(rx_v.at[pl.ds(0, paired), pl.ds(0, chunks * CHUNK)], wx_rs)
                 arrived(ra_v.at[:, pl.ds(0, chunks * CHUNK)], wa_rs)
                 for c in range(chunks):
                     rows, tokens = rows_at(c), rows_at(start + c)
-                    dx_v[EARLY, rows, :] = ra_v[EARLY, rows, :]
-                    for h in range(EARLY):
+                    if k:
+                        dx_v[EARLY, rows, :] = ra_v[EARLY, rows, :]
+                    for h in range(paired):
                         value = ra_v[h, rows, :].astype(jnp.float32) - rx_v[h, rows, :].astype(jnp.float32) * cb_v[tokens, :]
                         dx_v[h, rows, :] = value.astype(jnp.bfloat16)
                     (leg(c) if k else carry(c)).start()
@@ -359,8 +388,21 @@
             wrap_c(k).start()
 
     spread_columns(scalars, cb_v)
-    a_v[EARLY] = (dq_v[...] - x_v[EARLY].astype(jnp.float32) * cb_v[...]).astype(jnp.bfloat16)
-    pass_on(send_a, wrap_a, EARLY)
+    def complete(rows):
+        value = dq_v[rows, :] - x_v[EARLY, rows, :].astype(jnp.float32) * cb_v[rows, :]
+        a_v[EARLY, rows, :] = value.astype(jnp.bfloat16)
+
+    @pl.when(inland)
+    def _():
+        complete(lower)
+        send_a(EARLY, lower).start()
+
+    @pl.when(first)
+    def _():
+        for k in range(1, len(SHARES)):
+            start, chunks = SHARES[k]
+            complete(pl.ds(start * CHUNK, chunks * CHUNK))
+            wrap_a(EARLY, k).start()
 
     @pl.when(outer)
     def _():
@@ -384,7 +426,8 @@
 
     @pl.when(first)
     def _():
-        sent(x_ref, wx_ss)
+        sent(x_ref.at[pl.ds(0, 2 * EARLY)], wx_ss)
+        wrap_x(EARLY, 0, wl_ss).wait_send()
         sent(a_v, wa_ss)
         sent(inners_v.at[pl.ds(0, len(SHARES))], wc_ss)
 
@@ -415,33 +458,39 @@
 
     scalars_in = pltpu.make_async_copy(c_ref, c_v, in_s.at[3 * HEADS])
     scalars_in.start()
-    arrivals = [
-        [pltpu.make_async_copy(src.at[h], dst.at[h], in_s.at[k * HEADS + h])
-         for k, (src, dst) in enumerate(((lo_ref, lo_v), (a_ref, a_v), (x_ref, x_v))) if k < 2 or h < EARLY]
-        for h in range(HEADS)
-    ]
+    arrivals = []
+    for h in range(HEADS):
+        halves = pl.ds(2 * h, 2 if h < EARLY else 1)
+        arrivals.append([
+            pltpu.make_async_copy(lo_ref.at[h], lo_v.at[h], in_s.at[h]),
+            pltpu.make_async_copy(a_ref.at[h], a_v.at[h], in_s.at[HEADS + h]),
+            pltpu.make_async_copy(x_ref.at[halves], x_v.at[halves], in_s.at[2 * HEADS + h]),
+        ])
     for copies in arrivals:
-        for c in copies:
+        for c in copies[1:]:
             c.start()
+    for copies in arrivals:
+        copies[0].start()
+    leaving = []
     scalars_in.wait()
     spread_columns(c_v[...], cb_v)
-    leaving = []
     for h in range(HEADS):
-        for c in arrivals[h]:
+        for c in arrivals[h][1:]:
             c.wait()
+
+        @pl.when(jnp.logical_not(last))
+        def _():
+            for k in range(2 if h < EARLY else 1):
+                rows = pl.ds(k * HALF, HALF)
+                value = a_v[h, rows, :].astype(jnp.float32) - x_v[2 * h + k].astype(jnp.float32) * cb_v[rows, :]
+                a_v[h, rows, :] = value.astype(jnp.bfloat16)
+
+        made = pltpu.make_async_copy(a_v.at[h], columns(grad_ref, h), out_s.at[HEADS + h])
+        made.start()
+        arrivals[h][0].wait()
         passed_on = pltpu.make_async_copy(lo_v.at[h], columns(out_ref, h), out_s.at[h])
         passed_on.start()
-        leaving.append(passed_on)
-
-        if h < EARLY:
-            @pl.when(jnp.logical_not(last))
-            def _():
-                value = a_v[h].astype(jnp.float32) - x_v[h].astype(jnp.float32) * cb_v[...]
-                a_v[h] = value.astype(jnp.bfloat16)
-
-        made = pltpu.make_async_copy(a_v.at[h], columns(grad_ref, h), out_s.at[HEADS + h])
-        made.start()
-        leaving.append(made)
+        leaving += [made, passed_on]
     for c in leaving:
         c.wait()
 
@@ -456,7 +505,7 @@
     anywhere = pl.BlockSpec(memory_space=pl.ANY)
     flat = jax.ShapeDtypeStruct((SEQ, HEADS * HDIM), jnp.bfloat16)
     split = jax.ShapeDtypeStruct((HEADS, SEQ, HDIM), jnp.bfloat16)
-    early = jax.ShapeDtypeStruct((EARLY, SEQ, HDIM), jnp.bfloat16)
+    early = jax.ShapeDtypeStruct((2 * EARLY + 1, HALF, HDIM), jnp.bfloat16)
     lo, a, x, c = pl.pallas_call(
         kernel,
         out_shape=(split, split, early, jax.ShapeDtypeStruct((1, SEQ), jnp.float32)),
@@ -467,7 +516,7 @@
             pltpu.VMEM((1, 3 * SEQ), jnp.float32), pltpu.VMEM((GROUP, 1, 3 * SEQ), jnp.float32),
             row, row, row, pltpu.VMEM((GROUP, 1, SEQ), jnp.float32), row, column, column,
             pltpu.SemaphoreType.REGULAR, pltpu.SemaphoreType.REGULAR,
-        ] + [dma((2,))] + [dma] * 6 + [dma((HEADS,))] + [dma] * 21 + [dma((SHARES[0][1],))],
+        ] + [dma((2,))] + [dma] * 6 + [dma((HEADS,))] + [dma] * 22 + [dma((SHARES[0][1],))],
         compiler_params=pltpu.CompilerParams(collective_id=0, has_side_effects=True, vmem_limit_bytes=60 * 2**20),
         name="tick",
     )(eviction, layer_input[0], grad_input[0], stashed[0], query_gain, key_gain)
@@ -476,7 +525,7 @@
         out_shape=(flat, flat),
         in_specs=[anywhere] * 4,
         out_specs=(anywhere, anywhere),
-        scratch_shapes=[head_buffer] * 3 + [row, column, dma((3 * HEADS + 1,)), dma((2 * HEADS,))],
+        scratch_shapes=[head_buffer] * 2 + [pltpu.VMEM((2 * EARLY + 1, HALF, HDIM), jnp.bfloat16), row, column, dma((3 * HEADS + 1,)), dma((2 * HEADS,))],
         compiler_params=pltpu.CompilerParams(vmem_limit_bytes=60 * 2**20),
         name="finish",
     )(lo, a, x, c)

time: 47.4 us -> 46.2 us (0.975)
  the two profiles are of different devices: /device:TPU:640 before, /device:TPU:652 now
where the time goes in v6:
time: 46.2 us; the launch traced here: 46 us
  Pallas kernels  44.8 us (97%)
  between operations  1.28 us (3%)
    pallas_call x1, Pallas kernels, local(): pl.pallas_call(kernel, out_shape=(split, split, early, jax.ShapeDtypeStru...  42.6 us
    pallas_call x1, Pallas kernels, local(): pl.pallas_call(finish, out_shape=(flat, flat), in_specs=[anywhere] * 4, o...  2.2 us

profile of v6, /device:TPU:652, one launch (start us, length us, event | category | flops | bytes accessed | tf_op | source)
XLA Modules:
  0.0 46.0 jit_solution(16772725285479540495)
XLA Ops:
  1.3 42.6 %tick.1 = (bf16[3,512,128]{2,1,0:T(8,128)(2,1)}, bf16[3,512,128]{2,1,0:T(8,128)(2,1)}, bf16[5,256,128]{2,1,0:T(8,128)(2,1)}, f32[1,512]{1,0:T(1,128)}) custom-call(s32[1]{0:T(128)S(6)} %copy.8.ev_ref, bf16[512,384]{1,0:T(8,128)(2,1)} %bitcast.6, bf16[512,384]{1,0:T(8,128)(2,1)} %bitcast.7, bf16[2,512,384]{2,1,0:T(8,128)(2,1)} %bitcast.5, f32[1,384]{1,0:T(1,128)} %gq_ref.1, ...), custom_call_target="tpu_custom_call" | custom-call | tf_op jit(solution)/shard_map/tick/pallas_call | solution.py:509
  43.8 2.2 %finish.1 = (bf16[512,384]{1,0:T(8,128)(2,1)}, bf16[512,384]{1,0:T(8,128)(2,1)}) custom-call(bf16[3,512,128]{2,1,0:T(8,128)(2,1)} %get-tuple-element.8.lo_ref, bf16[3,512,128]{2,1,0:T(8,128)(2,1)} %get-tuple-element.9.a_ref, bf16[5,256,128]{2,1,0:T(8,128)(2,1)} %get-tuple-element.10.x_ref, f32[1,512]{1,0:T(1,128)} %get-tuple-element.11.c_ref), custom_call_target="tpu_custom_call" | custom-call | tf_op jit(solution)/shard_map/finish/pallas_call | solution.py:523
